TPU v7x, 256 devices: a whole 4x4x8 slice. The times are simulated.
256 devices in a mesh: ctx: 128 (over z, x_lo, y, core), head: 2 (over x_hi).
Axes of the slice: x: 4 (x_hi: 2, x_lo: 2; x = x_hi * 2 + x_lo), y: 4, z: 8, core: 2. Of those that a mesh axis runs over, the one named last changes fastest.
Arguments:
- latent_raw: bfloat16 [16384, 576], P(('ctx', 'head')), may hold values from -6 to 6
- kv_gain: float32 [512], replicated, may hold values from 0.1 to 1.9
- query_nope: bfloat16 [16384, 8192], P('ctx', 'head'), may hold values from -144 to 144
- query_rope: bfloat16 [16384, 4096], P('ctx', 'head'), may hold values from -6 to 6
- key_up: bfloat16 [64, 128, 512], P('head'), may hold values from -0.5 to 0.5
- value_up: bfloat16 [64, 512, 128], P('head'), may hold values from -0.25 to 0.25
- doc_lengths: int32 [32], replicated, may hold values from 1 to 896, 16384 in all
Outputs:
- attended: bfloat16 [16384, 8192], P('ctx', 'head')
Inputs may be any that keep to these rules, and one draw needn't show every extreme that they name: `doc_lengths`: documents lie end to end over all 16384 positions; the longest has exactly 896 positions.
All inputs are finite; a program needn't handle non-finite values.
Results may differ from a plain program's by a relative error of at most 0.012.
The roundings to bfloat16 on the way count: a program that leaves them out, or rounds other values in their place, can miss the bound.
Values may be sent and summed in bfloat16 or wider, within the bound.
A program may use at most 64 MiB of HBM per device.

v0:
```python
import jax
import jax.numpy as jnp
from jax import lax
from jax.sharding import PartitionSpec as P

HOPS = 7


epsilon = 1e-06
masked_score = -1e30


def shifted(value, axis, steps):
    count = lax.axis_size(axis)
    leading, last = (max(0, -steps), min(count, count - steps))
    return lax.ppermute(value, axis, [(source, source + steps) for source in range(leading, last)])


def doc_begin(positions, starts):
    inside = starts[None, :] <= positions[:, None]
    return jnp.max(jnp.where(inside, starts[None, :], 0), axis=1)


def rotation(offsets, rope_half):
    frequency = 10000.0 ** (-2.0 * jnp.arange(rope_half, dtype=jnp.float32) / (2 * rope_half))
    angles = offsets.astype(jnp.float32)[:, None] * frequency[None, :]
    return (jnp.cos(angles), jnp.sin(angles))


def rotate(values, cos_table, sin_table):
    rope_half = cos_table.shape[-1]
    first_half = values[..., :rope_half]
    second_half = values[..., rope_half:]
    return jnp.concatenate(
        [
            first_half * cos_table - second_half * sin_table,
            second_half * cos_table + first_half * sin_table,
        ],
        axis=-1,
    )


def shards(latent_raw, kv_gain, query_nope, query_rope, key_up, value_up, doc_lengths):
    row_count = query_nope.shape[0]
    head_count = key_up.shape[0]
    nope_width = key_up.shape[1]
    latent_width = key_up.shape[2]
    value_width = value_up.shape[2]
    full_width = latent_raw.shape[1]
    rope_width = full_width - latent_width
    rope_half = rope_width // 2
    half_rows = latent_raw.shape[0]
    score_scale = (nope_width + rope_width) ** (-0.5)
    ctx_index = lax.axis_index("ctx")
    head_index = lax.axis_index("head")
    starts = jnp.cumsum(doc_lengths) - doc_lengths
    own_pos = (
        ctx_index * row_count + head_index * half_rows + jnp.arange(half_rows, dtype=jnp.int32)
    )
    own_begin = doc_begin(own_pos, starts)
    cos_own, sin_own = rotation(own_pos - own_begin, rope_half)
    raw_rows = latent_raw.astype(jnp.float32)
    latent_part = raw_rows[:, :latent_width]
    normed = (
        latent_part
        * lax.rsqrt(jnp.mean(latent_part * latent_part, axis=1, keepdims=True) + epsilon)
        * kv_gain
    )
    kv_half = jnp.concatenate(
        [normed, rotate(raw_rows[:, latent_width:], cos_own, sin_own)], axis=1
    ).astype(jnp.bfloat16)
    flat_rows = lax.all_gather(kv_half.reshape(-1, 128), "head", axis=0, tiled=True)
    query_pos = ctx_index * row_count + jnp.arange(row_count, dtype=jnp.int32)
    query_begin = doc_begin(query_pos, starts)
    cos_query, sin_query = rotation(query_pos - query_begin, rope_half)
    absorbed = jnp.einsum(
        "thn,hnr->thr",
        query_nope.reshape(row_count, head_count, nope_width),
        key_up,
        preferred_element_type=jnp.float32,
    ).astype(jnp.bfloat16)
    rope_rows = query_rope.reshape(row_count, head_count, rope_width).astype(jnp.float32)
    rotated = rotate(rope_rows, cos_query[:, None, :], sin_query[:, None, :]).astype(jnp.bfloat16)
    queries = jnp.concatenate([absorbed, rotated], axis=2)

    def live_mask(first_pos):
        key_pos = first_pos + jnp.arange(row_count, dtype=jnp.int32)
        key_begin = doc_begin(key_pos, starts)
        return (
            (key_pos[None, :] <= query_pos[:, None])
            & (key_begin[None, :] == query_begin[:, None])
            & (key_pos[None, :] >= 0)
        )

    def attend(carry_state, key_flat, live_pairs):
        running_max, running_total, running_sum = carry_state
        key_block = key_flat.reshape(row_count, full_width)
        scores = (
            jnp.einsum("thc,sc->hts", queries, key_block, preferred_element_type=jnp.float32)
            * score_scale
        )
        scores = jnp.where(live_pairs[None], scores, masked_score)
        new_max = jnp.maximum(running_max, jnp.max(scores, axis=2))
        factor = jnp.exp(running_max - new_max)
        weights = jnp.where(live_pairs[None], jnp.exp(scores - new_max[:, :, None]), 0.0)
        new_total = running_total * factor + jnp.sum(weights, axis=2)
        new_sum = running_sum * factor[:, :, None] + jnp.einsum(
            "hts,sr->htr",
            weights.astype(jnp.bfloat16),
            key_block[:, :latent_width],
            preferred_element_type=jnp.float32,
        )
        return (new_max, new_total, new_sum)

    def visit_block(carry_state, key_flat, first_pos):
        live_pairs = live_mask(first_pos)
        return attend(carry_state, key_flat, live_pairs)

    start_state = (
        jnp.full((head_count, row_count), masked_score, jnp.float32),
        jnp.zeros((head_count, row_count), jnp.float32),
        jnp.zeros((head_count, row_count, latent_width), jnp.float32),
    )
    carry_state = visit_block(start_state, flat_rows, ctx_index * row_count)

    def hop_step(step_index, loop_carry):
        loop_state, moving = loop_carry
        moving = shifted(moving, "ctx", 1)
        loop_state = visit_block(loop_state, moving, (ctx_index - 1 - step_index) * row_count)
        return (loop_state, moving)

    carry_state, unused = lax.fori_loop(0, HOPS, hop_step, (carry_state, flat_rows))
    running_max, running_total, running_sum = carry_state
    mixed_latent = (running_sum / running_total[:, :, None]).astype(jnp.bfloat16)
    attended = jnp.einsum(
        "htr,hrv->thv", mixed_latent, value_up, preferred_element_type=jnp.float32
    )
    return attended.astype(jnp.bfloat16).reshape(row_count, head_count * value_width)


def solution(mesh):
    return jax.shard_map(
        shards,
        mesh=mesh,
        in_specs=(
            P(("ctx", "head"), None),
            P(),
            P("ctx", "head"),
            P("ctx", "head"),
            P("head", None, None),
            P("head", None, None),
            P(),
        ),
        out_specs=P("ctx", "head"),
        check_vma=False,
    )
```

profile of v0, /device:TPU:128, one launch (start us, length us, event | category | flops | bytes accessed | tf_op | source)
XLA Modules:
  0.0 183.4 jit_solution(4096299263825713121)
XLA Ops:
  4.2 6.5 %all_gather.3 = bf16[576,128]{1,0:T(8,128)(2,1)S(1)} all-gather(bf16[288,128]{1,0:T(8,128)(2,1)S(1)} %convert_element_type.58), channel_id=1, replica_groups=mesh['ctx'=128,'head'=2] {'head'}, dimensions={0}, use_global_device_ids=true | all-gather | bytes 221184 | tf_op jit(solution)/shard_map/all_gather | solution.py:72
  12.7 3.5 %convert_bitcast_fusion = bf16[128,32,512]{0,2,1:T(8,128)(2,1)S(1)} fusion(bf16[32,128,512]{2,1,0:T(8,128)(2,1)} %param.13, bf16[128,4096]{1,0:T(8,128)(2,1)S(1)} %copy-done), kind=kOutput, calls=%fused_computation.28 | convolution fusion | flops 538968064 | bytes 9437184 | tf_op jit(solution)/shard_map/thn,hnr->thr/dot_general | solution.py:76
  17.9 4.0 %broadcast_add_fusion = f32[32,128,512]{2,1,0:T(8,128)} fusion(f32[32,128]{1,0:T(8,128)S(1)} %get-tuple-element.295, f32[128,128,32]{1,0,2:T(8,128)S(1)} %get-tuple-element.300, f32[32,128]{1,0:T(8,128)S(1)} %broadcast_maximum_fusion, pred[128,128]{0,1:T(8,128)(4,1)S(1)} %and_and_fusion.1, bf16[128,576]{1,0:T(8,128)(2,1)S(1)} %reshape.310), kind=kOutput, calls=%fused_computation.27 | convolution fusion | flops 541589504 | bytes 10665984 | tf_op jit(solution)/shard_map/hts,sr->htr/dot_general | solution.py:107
  24.3 151.2 %while.22 = (s32[]{:T(128)}, f32[32,128]{1,0:T(8,128)S(1)}, f32[32,128]{1,0:T(8,128)S(1)}, f32[32,128,512]{2,1,0:T(8,128)}, bf16[576,128]{1,0:T(8,128)(2,1)S(1)}...) while((s32[]{:T(128)}, f32[32,128]{1,0:T(8,128)S(1)}, ...), condition=%wide.region_10.11_spmd.clone, body=%wide.region_6.10_spmd.clone.sunk | while | flops 1151947136 | bytes 96686712 | solution.py:132
  26.5 8.5 %collective-permute-done = bf16[576,128]{1,0:T(8,128)(2,1)S(1)} collective-permute-done((bf16[576,128]{1,0:T(8,128)(2,1)S(1)}, bf16[576,128]{1,0:T(8,128)(2,1)S(1)}, u32[]{:S(2)}, u32[]{:S(2)}) %collective-permute-start) | collective-permute-done | bytes 147488 | tf_op jit(solution)/shard_map/while/body/eval_jaxpr/ppermute | solution.py:16
  35.2 3.6 %fusion.53 = (f32[32,128]{1,0:T(8,128)S(1)}, f32[128,128,32]{1,0,2:T(8,128)S(1)}) fusion(pred[128,128]{0,1:T(8,128)(4,1)S(1)} %and_and_fusion.3, bf16[128,32,576]{0,2,1:T(8,128)(2,1)} %get-tuple-element.406, bf16[128,576]{1,0:T(8,128)(2,1)S(1)} %reshape.321), kind=kOutput, calls=%fused_computation.4.clone.1 | convolution fusion | flops 605548544 | bytes 6995968 | tf_op jit(solution)/shard_map/while/body/eval_jaxpr/thc,sc->hts/dot_general | solution.py:99
  40.0 2.7 %multiply_add_fusion.5 = f32[32,128,512]{2,1,0:T(8,128)S(1)} fusion(f32[32,128,512]{2,1,0:T(8,128)S(1)} %copy-done.1, f32[32,128]{1,0:T(8,128)S(1)} %get-tuple-element.373, f32[128,128,32]{1,0,2:T(8,128)S(1)} %get-tuple-element.371, f32[32,128]{1,0:T(8,128)S(1)} %max.11, pred[128,128]{0,1:T(8,128)(4,1)S(1)} %and_and_fusion.3, ...), kind=kOutput, calls=%fused_computation.1.clone.1 | convolution fusion | flops 543686656 | bytes 19054592 | tf_op jit(solution)/shard_map/while/body/eval_jaxpr/hts,sr->htr/dot_general | solution.py:107
  42.7 3.2 %copy-done.2 = f32[32,128,512]{2,1,0:T(8,128)} copy-done((f32[32,128,512]{2,1,0:T(8,128)}, f32[32,128,512]{2,1,0:T(8,128)S(1)}, u32[]{:S(2)}) %copy-start.2) | copy-done | bytes 8388632 | tf_op jit(solution)/shard_map/while
  48.1 8.5 %collective-permute-done = bf16[576,128]{1,0:T(8,128)(2,1)S(1)} collective-permute-done((bf16[576,128]{1,0:T(8,128)(2,1)S(1)}, bf16[576,128]{1,0:T(8,128)(2,1)S(1)}, u32[]{:S(2)}, u32[]{:S(2)}) %collective-permute-start) | collective-permute-done | bytes 147488 | tf_op jit(solution)/shard_map/while/body/eval_jaxpr/ppermute | solution.py:16
  56.8 3.6 %fusion.53 = (f32[32,128]{1,0:T(8,128)S(1)}, f32[128,128,32]{1,0,2:T(8,128)S(1)}) fusion(pred[128,128]{0,1:T(8,128)(4,1)S(1)} %and_and_fusion.3, bf16[128,32,576]{0,2,1:T(8,128)(2,1)} %get-tuple-element.406, bf16[128,576]{1,0:T(8,128)(2,1)S(1)} %reshape.321), kind=kOutput, calls=%fused_computation.4.clone.1 | convolution fusion | flops 605548544 | bytes 6995968 | tf_op jit(solution)/shard_map/while/body/eval_jaxpr/thc,sc->hts/dot_general | solution.py:99
  61.6 2.7 %multiply_add_fusion.5 = f32[32,128,512]{2,1,0:T(8,128)S(1)} fusion(f32[32,128,512]{2,1,0:T(8,128)S(1)} %copy-done.1, f32[32,128]{1,0:T(8,128)S(1)} %get-tuple-element.373, f32[128,128,32]{1,0,2:T(8,128)S(1)} %get-tuple-element.371, f32[32,128]{1,0:T(8,128)S(1)} %max.11, pred[128,128]{0,1:T(8,128)(4,1)S(1)} %and_and_fusion.3, ...), kind=kOutput, calls=%fused_computation.1.clone.1 | convolution fusion | flops 543686656 | bytes 19054592 | tf_op jit(solution)/shard_map/while/body/eval_jaxpr/hts,sr->htr/dot_general | solution.py:107
  64.3 3.2 %copy-done.2 = f32[32,128,512]{2,1,0:T(8,128)} copy-done((f32[32,128,512]{2,1,0:T(8,128)}, f32[32,128,512]{2,1,0:T(8,128)S(1)}, u32[]{:S(2)}) %copy-start.2) | copy-done | bytes 8388632 | tf_op jit(solution)/shard_map/while
  69.7 8.5 %collective-permute-done = bf16[576,128]{1,0:T(8,128)(2,1)S(1)} collective-permute-done((bf16[576,128]{1,0:T(8,128)(2,1)S(1)}, bf16[576,128]{1,0:T(8,128)(2,1)S(1)}, u32[]{:S(2)}, u32[]{:S(2)}) %collective-permute-start) | collective-permute-done | bytes 147488 | tf_op jit(solution)/shard_map/while/body/eval_jaxpr/ppermute | solution.py:16
  78.4 3.6 %fusion.53 = (f32[32,128]{1,0:T(8,128)S(1)}, f32[128,128,32]{1,0,2:T(8,128)S(1)}) fusion(pred[128,128]{0,1:T(8,128)(4,1)S(1)} %and_and_fusion.3, bf16[128,32,576]{0,2,1:T(8,128)(2,1)} %get-tuple-element.406, bf16[128,576]{1,0:T(8,128)(2,1)S(1)} %reshape.321), kind=kOutput, calls=%fused_computation.4.clone.1 | convolution fusion | flops 605548544 | bytes 6995968 | tf_op jit(solution)/shard_map/while/body/eval_jaxpr/thc,sc->hts/dot_general | solution.py:99
  83.2 2.7 %multiply_add_fusion.5 = f32[32,128,512]{2,1,0:T(8,128)S(1)} fusion(f32[32,128,512]{2,1,0:T(8,128)S(1)} %copy-done.1, f32[32,128]{1,0:T(8,128)S(1)} %get-tuple-element.373, f32[128,128,32]{1,0,2:T(8,128)S(1)} %get-tuple-element.371, f32[32,128]{1,0:T(8,128)S(1)} %max.11, pred[128,128]{0,1:T(8,128)(4,1)S(1)} %and_and_fusion.3, ...), kind=kOutput, calls=%fused_computation.1.clone.1 | convolution fusion | flops 543686656 | bytes 19054592 | tf_op jit(solution)/shard_map/while/body/eval_jaxpr/hts,sr->htr/dot_general | solution.py:107
  85.9 3.2 %copy-done.2 = f32[32,128,512]{2,1,0:T(8,128)} copy-done((f32[32,128,512]{2,1,0:T(8,128)}, f32[32,128,512]{2,1,0:T(8,128)S(1)}, u32[]{:S(2)}) %copy-start.2) | copy-done | bytes 8388632 | tf_op jit(solution)/shard_map/while
  91.3 8.5 %collective-permute-done = bf16[576,128]{1,0:T(8,128)(2,1)S(1)} collective-permute-done((bf16[576,128]{1,0:T(8,128)(2,1)S(1)}, bf16[576,128]{1,0:T(8,128)(2,1)S(1)}, u32[]{:S(2)}, u32[]{:S(2)}) %collective-permute-start) | collective-permute-done | bytes 147488 | tf_op jit(solution)/shard_map/while/body/eval_jaxpr/ppermute | solution.py:16
  100.0 3.6 %fusion.53 = (f32[32,128]{1,0:T(8,128)S(1)}, f32[128,128,32]{1,0,2:T(8,128)S(1)}) fusion(pred[128,128]{0,1:T(8,128)(4,1)S(1)} %and_and_fusion.3, bf16[128,32,576]{0,2,1:T(8,128)(2,1)} %get-tuple-element.406, bf16[128,576]{1,0:T(8,128)(2,1)S(1)} %reshape.321), kind=kOutput, calls=%fused_computation.4.clone.1 | convolution fusion | flops 605548544 | bytes 6995968 | tf_op jit(solution)/shard_map/while/body/eval_jaxpr/thc,sc->hts/dot_general | solution.py:99
  104.8 2.7 %multiply_add_fusion.5 = f32[32,128,512]{2,1,0:T(8,128)S(1)} fusion(f32[32,128,512]{2,1,0:T(8,128)S(1)} %copy-done.1, f32[32,128]{1,0:T(8,128)S(1)} %get-tuple-element.373, f32[128,128,32]{1,0,2:T(8,128)S(1)} %get-tuple-element.371, f32[32,128]{1,0:T(8,128)S(1)} %max.11, pred[128,128]{0,1:T(8,128)(4,1)S(1)} %and_and_fusion.3, ...), kind=kOutput, calls=%fused_computation.1.clone.1 | convolution fusion | flops 543686656 | bytes 19054592 | tf_op jit(solution)/shard_map/while/body/eval_jaxpr/hts,sr->htr/dot_general | solution.py:107
  107.5 3.2 %copy-done.2 = f32[32,128,512]{2,1,0:T(8,128)} copy-done((f32[32,128,512]{2,1,0:T(8,128)}, f32[32,128,512]{2,1,0:T(8,128)S(1)}, u32[]{:S(2)}) %copy-start.2) | copy-done | bytes 8388632 | tf_op jit(solution)/shard_map/while
  112.9 8.5 %collective-permute-done = bf16[576,128]{1,0:T(8,128)(2,1)S(1)} collective-permute-done((bf16[576,128]{1,0:T(8,128)(2,1)S(1)}, bf16[576,128]{1,0:T(8,128)(2,1)S(1)}, u32[]{:S(2)}, u32[]{:S(2)}) %collective-permute-start) | collective-permute-done | bytes 147488 | tf_op jit(solution)/shard_map/while/body/eval_jaxpr/ppermute | solution.py:16
  121.6 3.6 %fusion.53 = (f32[32,128]{1,0:T(8,128)S(1)}, f32[128,128,32]{1,0,2:T(8,128)S(1)}) fusion(pred[128,128]{0,1:T(8,128)(4,1)S(1)} %and_and_fusion.3, bf16[128,32,576]{0,2,1:T(8,128)(2,1)} %get-tuple-element.406, bf16[128,576]{1,0:T(8,128)(2,1)S(1)} %reshape.321), kind=kOutput, calls=%fused_computation.4.clone.1 | convolution fusion | flops 605548544 | bytes 6995968 | tf_op jit(solution)/shard_map/while/body/eval_jaxpr/thc,sc->hts/dot_general | solution.py:99
  126.4 2.7 %multiply_add_fusion.5 = f32[32,128,512]{2,1,0:T(8,128)S(1)} fusion(f32[32,128,512]{2,1,0:T(8,128)S(1)} %copy-done.1, f32[32,128]{1,0:T(8,128)S(1)} %get-tuple-element.373, f32[128,128,32]{1,0,2:T(8,128)S(1)} %get-tuple-element.371, f32[32,128]{1,0:T(8,128)S(1)} %max.11, pred[128,128]{0,1:T(8,128)(4,1)S(1)} %and_and_fusion.3, ...), kind=kOutput, calls=%fused_computation.1.clone.1 | convolution fusion | flops 543686656 | bytes 19054592 | tf_op jit(solution)/shard_map/while/body/eval_jaxpr/hts,sr->htr/dot_general | solution.py:107
  129.1 3.2 %copy-done.2 = f32[32,128,512]{2,1,0:T(8,128)} copy-done((f32[32,128,512]{2,1,0:T(8,128)}, f32[32,128,512]{2,1,0:T(8,128)S(1)}, u32[]{:S(2)}) %copy-start.2) | copy-done | bytes 8388632 | tf_op jit(solution)/shard_map/while
  134.5 8.5 %collective-permute-done = bf16[576,128]{1,0:T(8,128)(2,1)S(1)} collective-permute-done((bf16[576,128]{1,0:T(8,128)(2,1)S(1)}, bf16[576,128]{1,0:T(8,128)(2,1)S(1)}, u32[]{:S(2)}, u32[]{:S(2)}) %collective-permute-start) | collective-permute-done | bytes 147488 | tf_op jit(solution)/shard_map/while/body/eval_jaxpr/ppermute | solution.py:16
  143.2 3.6 %fusion.53 = (f32[32,128]{1,0:T(8,128)S(1)}, f32[128,128,32]{1,0,2:T(8,128)S(1)}) fusion(pred[128,128]{0,1:T(8,128)(4,1)S(1)} %and_and_fusion.3, bf16[128,32,576]{0,2,1:T(8,128)(2,1)} %get-tuple-element.406, bf16[128,576]{1,0:T(8,128)(2,1)S(1)} %reshape.321), kind=kOutput, calls=%fused_computation.4.clone.1 | convolution fusion | flops 605548544 | bytes 6995968 | tf_op jit(solution)/shard_map/while/body/eval_jaxpr/thc,sc->hts/dot_general | solution.py:99
  150.7 3.2 %copy-done.2 = f32[32,128,512]{2,1,0:T(8,128)} copy-done((f32[32,128,512]{2,1,0:T(8,128)}, f32[32,128,512]{2,1,0:T(8,128)S(1)}, u32[]{:S(2)}) %copy-start.2) | copy-done | bytes 8388632 | tf_op jit(solution)/shard_map/while
  156.1 8.5 %collective-permute-done = bf16[576,128]{1,0:T(8,128)(2,1)S(1)} collective-permute-done((bf16[576,128]{1,0:T(8,128)(2,1)S(1)}, bf16[576,128]{1,0:T(8,128)(2,1)S(1)}, u32[]{:S(2)}, u32[]{:S(2)}) %collective-permute-start) | collective-permute-done | bytes 147488 | tf_op jit(solution)/shard_map/while/body/eval_jaxpr/ppermute | solution.py:16
  164.8 3.6 %fusion.53 = (f32[32,128]{1,0:T(8,128)S(1)}, f32[128,128,32]{1,0,2:T(8,128)S(1)}) fusion(pred[128,128]{0,1:T(8,128)(4,1)S(1)} %and_and_fusion.3, bf16[128,32,576]{0,2,1:T(8,128)(2,1)} %get-tuple-element.406, bf16[128,576]{1,0:T(8,128)(2,1)S(1)} %reshape.321), kind=kOutput, calls=%fused_computation.4.clone.1 | convolution fusion | flops 605548544 | bytes 6995968 | tf_op jit(solution)/shard_map/while/body/eval_jaxpr/thc,sc->hts/dot_general | solution.py:99
  169.6 2.7 %multiply_add_fusion.5 = f32[32,128,512]{2,1,0:T(8,128)S(1)} fusion(f32[32,128,512]{2,1,0:T(8,128)S(1)} %copy-done.1, f32[32,128]{1,0:T(8,128)S(1)} %get-tuple-element.373, f32[128,128,32]{1,0,2:T(8,128)S(1)} %get-tuple-element.371, f32[32,128]{1,0:T(8,128)S(1)} %max.11, pred[128,128]{0,1:T(8,128)(4,1)S(1)} %and_and_fusion.3, ...), kind=kOutput, calls=%fused_computation.1.clone.1 | convolution fusion | flops 543686656 | bytes 19054592 | tf_op jit(solution)/shard_map/while/body/eval_jaxpr/hts,sr->htr/dot_general | solution.py:107
  172.3 3.2 %copy-done.2 = f32[32,128,512]{2,1,0:T(8,128)} copy-done((f32[32,128,512]{2,1,0:T(8,128)}, f32[32,128,512]{2,1,0:T(8,128)S(1)}, u32[]{:S(2)}) %copy-start.2) | copy-done | bytes 8388632 | tf_op jit(solution)/shard_map/while
  175.5 6.5 %fusion.18 = bf16[32,128,128]{1,2,0:T(8,128)(2,1)S(1)} fusion(bf16[32,512,128]{2,1,0:T(8,128)(2,1)} %param.14, f32[32,128,512]{2,1,0:T(8,128)} %get-tuple-element.240, f32[32,128]{1,0:T(8,128)S(1)} %get-tuple-element.241), kind=kOutput, calls=%fused_computation.33 | convolution fusion | flops 541589504 | bytes 13647872 | tf_op jit(solution)/shard_map/htr,hrv->thv/dot_general | solution.py:135
  (133 shorter events, 38.7 us)
Async XLA Ops:
  0.0 12.7 %copy-start = (bf16[128,4096]{1,0:T(8,128)(2,1)S(1)}, bf16[128,4096]{1,0:T(8,128)(2,1)}, u32[]{:S(2)}) copy-start(bf16[128,4096]{1,0:T(8,128)(2,1)} %param.11) | copy-start | bytes 3145732
  24.3 10.7 %collective-permute-start = (bf16[576,128]{1,0:T(8,128)(2,1)S(1)}, bf16[576,128]{1,0:T(8,128)(2,1)S(1)}, u32[]{:S(2)}, u32[]{:S(2)}) collective-permute-start(bf16[576,128]{1,0:T(8,128)(2,1)S(1)} %get-tuple-element.390), channel_id=1, source_target_pairs={{0,2},{2,4},{4,6},{6,8},{8,10},{10,12},{12,14},{14,16},{16,18},{18... | collective-permute-start | bytes 442376 | tf_op jit(solution)/shard_map/while/body/eval_jaxpr/ppermute | solution.py:16
  35.2 4.8 %copy-start.1 = (f32[32,128,512]{2,1,0:T(8,128)S(1)}, f32[32,128,512]{2,1,0:T(8,128)}, u32[]{:S(2)}) copy-start(f32[32,128,512]{2,1,0:T(8,128)} %get-tuple-element.389) | copy-start | bytes 25165828 | tf_op jit(solution)/shard_map/while
  42.7 3.2 %copy-start.2 = (f32[32,128,512]{2,1,0:T(8,128)}, f32[32,128,512]{2,1,0:T(8,128)S(1)}, u32[]{:S(2)}) copy-start(f32[32,128,512]{2,1,0:T(8,128)S(1)} %multiply_add_fusion.5) | copy-start | bytes 25165828 | tf_op jit(solution)/shard_map/while
  45.9 10.7 %collective-permute-start = (bf16[576,128]{1,0:T(8,128)(2,1)S(1)}, bf16[576,128]{1,0:T(8,128)(2,1)S(1)}, u32[]{:S(2)}, u32[]{:S(2)}) collective-permute-start(bf16[576,128]{1,0:T(8,128)(2,1)S(1)} %get-tuple-element.390), channel_id=1, source_target_pairs={{0,2},{2,4},{4,6},{6,8},{8,10},{10,12},{12,14},{14,16},{16,18},{18... | collective-permute-start | bytes 442376 | tf_op jit(solution)/shard_map/while/body/eval_jaxpr/ppermute | solution.py:16
  56.8 4.8 %copy-start.1 = (f32[32,128,512]{2,1,0:T(8,128)S(1)}, f32[32,128,512]{2,1,0:T(8,128)}, u32[]{:S(2)}) copy-start(f32[32,128,512]{2,1,0:T(8,128)} %get-tuple-element.389) | copy-start | bytes 25165828 | tf_op jit(solution)/shard_map/while
  64.3 3.2 %copy-start.2 = (f32[32,128,512]{2,1,0:T(8,128)}, f32[32,128,512]{2,1,0:T(8,128)S(1)}, u32[]{:S(2)}) copy-start(f32[32,128,512]{2,1,0:T(8,128)S(1)} %multiply_add_fusion.5) | copy-start | bytes 25165828 | tf_op jit(solution)/shard_map/while
  67.5 10.7 %collective-permute-start = (bf16[576,128]{1,0:T(8,128)(2,1)S(1)}, bf16[576,128]{1,0:T(8,128)(2,1)S(1)}, u32[]{:S(2)}, u32[]{:S(2)}) collective-permute-start(bf16[576,128]{1,0:T(8,128)(2,1)S(1)} %get-tuple-element.390), channel_id=1, source_target_pairs={{0,2},{2,4},{4,6},{6,8},{8,10},{10,12},{12,14},{14,16},{16,18},{18... | collective-permute-start | bytes 442376 | tf_op jit(solution)/shard_map/while/body/eval_jaxpr/ppermute | solution.py:16
  78.4 4.8 %copy-start.1 = (f32[32,128,512]{2,1,0:T(8,128)S(1)}, f32[32,128,512]{2,1,0:T(8,128)}, u32[]{:S(2)}) copy-start(f32[32,128,512]{2,1,0:T(8,128)} %get-tuple-element.389) | copy-start | bytes 25165828 | tf_op jit(solution)/shard_map/while
  85.9 3.2 %copy-start.2 = (f32[32,128,512]{2,1,0:T(8,128)}, f32[32,128,512]{2,1,0:T(8,128)S(1)}, u32[]{:S(2)}) copy-start(f32[32,128,512]{2,1,0:T(8,128)S(1)} %multiply_add_fusion.5) | copy-start | bytes 25165828 | tf_op jit(solution)/shard_map/while
  89.1 10.7 %collective-permute-start = (bf16[576,128]{1,0:T(8,128)(2,1)S(1)}, bf16[576,128]{1,0:T(8,128)(2,1)S(1)}, u32[]{:S(2)}, u32[]{:S(2)}) collective-permute-start(bf16[576,128]{1,0:T(8,128)(2,1)S(1)} %get-tuple-element.390), channel_id=1, source_target_pairs={{0,2},{2,4},{4,6},{6,8},{8,10},{10,12},{12,14},{14,16},{16,18},{18... | collective-permute-start | bytes 442376 | tf_op jit(solution)/shard_map/while/body/eval_jaxpr/ppermute | solution.py:16
  100.0 4.8 %copy-start.1 = (f32[32,128,512]{2,1,0:T(8,128)S(1)}, f32[32,128,512]{2,1,0:T(8,128)}, u32[]{:S(2)}) copy-start(f32[32,128,512]{2,1,0:T(8,128)} %get-tuple-element.389) | copy-start | bytes 25165828 | tf_op jit(solution)/shard_map/while
  107.5 3.2 %copy-start.2 = (f32[32,128,512]{2,1,0:T(8,128)}, f32[32,128,512]{2,1,0:T(8,128)S(1)}, u32[]{:S(2)}) copy-start(f32[32,128,512]{2,1,0:T(8,128)S(1)} %multiply_add_fusion.5) | copy-start | bytes 25165828 | tf_op jit(solution)/shard_map/while
  110.7 10.7 %collective-permute-start = (bf16[576,128]{1,0:T(8,128)(2,1)S(1)}, bf16[576,128]{1,0:T(8,128)(2,1)S(1)}, u32[]{:S(2)}, u32[]{:S(2)}) collective-permute-start(bf16[576,128]{1,0:T(8,128)(2,1)S(1)} %get-tuple-element.390), channel_id=1, source_target_pairs={{0,2},{2,4},{4,6},{6,8},{8,10},{10,12},{12,14},{14,16},{16,18},{18... | collective-permute-start | bytes 442376 | tf_op jit(solution)/shard_map/while/body/eval_jaxpr/ppermute | solution.py:16
  121.6 4.8 %copy-start.1 = (f32[32,128,512]{2,1,0:T(8,128)S(1)}, f32[32,128,512]{2,1,0:T(8,128)}, u32[]{:S(2)}) copy-start(f32[32,128,512]{2,1,0:T(8,128)} %get-tuple-element.389) | copy-start | bytes 25165828 | tf_op jit(solution)/shard_map/while
  129.1 3.2 %copy-start.2 = (f32[32,128,512]{2,1,0:T(8,128)}, f32[32,128,512]{2,1,0:T(8,128)S(1)}, u32[]{:S(2)}) copy-start(f32[32,128,512]{2,1,0:T(8,128)S(1)} %multiply_add_fusion.5) | copy-start | bytes 25165828 | tf_op jit(solution)/shard_map/while
  132.3 10.7 %collective-permute-start = (bf16[576,128]{1,0:T(8,128)(2,1)S(1)}, bf16[576,128]{1,0:T(8,128)(2,1)S(1)}, u32[]{:S(2)}, u32[]{:S(2)}) collective-permute-start(bf16[576,128]{1,0:T(8,128)(2,1)S(1)} %get-tuple-element.390), channel_id=1, source_target_pairs={{0,2},{2,4},{4,6},{6,8},{8,10},{10,12},{12,14},{14,16},{16,18},{18... | collective-permute-start | bytes 442376 | tf_op jit(solution)/shard_map/while/body/eval_jaxpr/ppermute | solution.py:16
  143.2 4.8 %copy-start.1 = (f32[32,128,512]{2,1,0:T(8,128)S(1)}, f32[32,128,512]{2,1,0:T(8,128)}, u32[]{:S(2)}) copy-start(f32[32,128,512]{2,1,0:T(8,128)} %get-tuple-element.389) | copy-start | bytes 25165828 | tf_op jit(solution)/shard_map/while
  150.7 3.2 %copy-start.2 = (f32[32,128,512]{2,1,0:T(8,128)}, f32[32,128,512]{2,1,0:T(8,128)S(1)}, u32[]{:S(2)}) copy-start(f32[32,128,512]{2,1,0:T(8,128)S(1)} %multiply_add_fusion.5) | copy-start | bytes 25165828 | tf_op jit(solution)/shard_map/while
  153.9 10.7 %collective-permute-start = (bf16[576,128]{1,0:T(8,128)(2,1)S(1)}, bf16[576,128]{1,0:T(8,128)(2,1)S(1)}, u32[]{:S(2)}, u32[]{:S(2)}) collective-permute-start(bf16[576,128]{1,0:T(8,128)(2,1)S(1)} %get-tuple-element.390), channel_id=1, source_target_pairs={{0,2},{2,4},{4,6},{6,8},{8,10},{10,12},{12,14},{14,16},{16,18},{18... | collective-permute-start | bytes 442376 | tf_op jit(solution)/shard_map/while/body/eval_jaxpr/ppermute | solution.py:16
  164.8 4.8 %copy-start.1 = (f32[32,128,512]{2,1,0:T(8,128)S(1)}, f32[32,128,512]{2,1,0:T(8,128)}, u32[]{:S(2)}) copy-start(f32[32,128,512]{2,1,0:T(8,128)} %get-tuple-element.389) | copy-start | bytes 25165828 | tf_op jit(solution)/shard_map/while
  172.3 3.2 %copy-start.2 = (f32[32,128,512]{2,1,0:T(8,128)}, f32[32,128,512]{2,1,0:T(8,128)S(1)}, u32[]{:S(2)}) copy-start(f32[32,128,512]{2,1,0:T(8,128)S(1)} %multiply_add_fusion.5) | copy-start | bytes 25165828 | tf_op jit(solution)/shard_map/while
where the time goes:
time: 184 us; the launch traced here: 183 us
  waiting for transfers between devices  59.6 us (32%)
  matrix products  59.2 us (32%)
  local copies, waits for them, and re-layouts  32.7 us (18%)
  starting transfers between devices  13.4 us (7%)
  other arithmetic  11.1 us (6%)
  blocking collectives  6.53 us (4%)
    ppermute x7, waiting for transfers between devices, shifted(): lax.ppermute(value, axis, [(source, source + steps) for source in range(l...  59.6 us
    while x42, local copies, waits for them, and re-layouts  26.8 us
    dot_general x8, matrix products, attend(): jnp.einsum('thc,sc->hts', queries, key_block, preferred_element_type=jnp....  26 us
    dot_general x8, matrix products, attend(): jnp.einsum('hts,sr->htr', weights.astype(jnp.bfloat16), key_block[:, :lat...  23.2 us
    ppermute x7, starting transfers between devices, shifted(): lax.ppermute(value, axis, [(source, source + steps) for source in range(l...  13.4 us
    dot_general x1, matrix products, shards(): jnp.einsum('htr,hrv->thv', mixed_latent, value_up, preferred_element_type...  6.54 us
    all_gather x1, blocking collectives, shards(): lax.all_gather(kv_half.reshape(-1, 128), 'head', axis=0, tiled=True)  6.53 us
    reduce_sum x8, other arithmetic, attend(): new_total = running_total * factor + jnp.sum(weights, axis=2)  4.48 us
  transfers between devices with their start and end apart: 7, of which 7 were waited for; matrix products, arithmetic and copies ran while one was open for 1% of the time, Pallas kernels for 0%

commit v1 on v0

v1 whole, which is shorter than its diff:
```python
import functools
import math

import jax
import jax.numpy as jnp
from jax import lax
from jax.experimental import pallas as pl
from jax.experimental.pallas import tpu as pltpu
from jax.sharding import PartitionSpec as P

LATENT, WIDTH = 512, 640
ROWS, HALF, BLOCKS, DOCS = 128, 64, 8, 32
KEYS = BLOCKS * ROWS
SCALE = 192.0 ** -0.5
LOG2E = math.log2(math.e)
DIRECT = (2, 4, 6)
MESH = pl.DeviceIdType.MESH


def gather_kernel(count, raw_ref, gain_ref, len_ref, kv_ref, begin_ref, cos_ref, sin_ref, send_sem, recv_sem):
    ctx, head = lax.axis_index("ctx"), lax.axis_index("head")
    core = lax.rem(ctx, 2)
    other = 1 - head
    sibling = ctx + 1 - 2 * core

    def later(steps):
        return lax.rem(ctx + steps, count)

    def earlier(steps):
        return lax.rem(ctx + count - steps, count)

    barrier = pltpu.get_barrier_semaphore()

    def greet(where):
        pl.semaphore_signal(barrier, inc=1, device_id=where, device_id_type=MESH)

    greet((ctx, other))
    greet((sibling, head))
    for steps in DIRECT:
        greet((earlier(steps), head))

    @pl.when(core == 0)
    def _():
        greet((earlier(7), head))

    row = lax.broadcasted_iota(jnp.int32, (ROWS, 128), 0)
    lane = lax.broadcasted_iota(jnp.int32, (ROWS, 128), 1)
    position = ctx * ROWS + row
    begin = jnp.zeros((ROWS, 128), jnp.int32)
    start = jnp.int32(0)
    for doc in range(DOCS):
        begin = jnp.where(position >= start, start, begin)
        start = start + len_ref[doc]
    begin_ref[...] = begin
    frequency = jnp.exp2((lane & 31).astype(jnp.float32) * (-math.log2(10000.0) / 32))
    angle = (position - begin).astype(jnp.float32) * frequency
    cos_ref[...] = jnp.cos(angle)
    sine = jnp.sin(angle)
    sin_ref[...] = jnp.where((lane & 63) < 32, -sine, sine)

    def place(steps, half):
        return pl.ds((BLOCKS - 1 - steps) * ROWS + half * HALF, HALF)

    mine = pl.ds((BLOCKS - 1) * ROWS + pl.multiple_of(head * HALF, HALF), HALF)
    latent = raw_ref[:, :LATENT].astype(jnp.float32)
    norm = lax.rsqrt(jnp.mean(latent * latent, axis=1, keepdims=True) + 1e-6)
    kv_ref[mine, :LATENT] = (latent * norm * gain_ref[...]).astype(jnp.bfloat16)
    rope = raw_ref[:, LATENT:].astype(jnp.float32)
    swapped = jnp.concatenate([rope[:, 32:], rope[:, :32]], axis=1)
    table = pl.ds(pl.multiple_of(head * HALF, HALF), HALF)
    turned = rope * cos_ref[table, :64] + swapped * sin_ref[table, :64]
    kv_ref[mine, LATENT:] = jnp.concatenate([turned, turned], axis=1).astype(jnp.bfloat16)

    pl.semaphore_wait(barrier, 5 + core)

    def half_at(steps, half):
        first = (BLOCKS - 1 - steps) * ROWS
        return pl.ds(first + pl.multiple_of(half * HALF, HALF), HALF)

    def copy(source, target, half, where):
        return pltpu.make_async_remote_copy(
            src_ref=kv_ref.at[half_at(source, half)],
            dst_ref=kv_ref.at[half_at(target, half)],
            send_sem=send_sem.at[target, half],
            recv_sem=recv_sem.at[target, half],
            device_id=where,
            device_id_type=MESH,
        )

    def to_partner():
        return copy(0, 0, head, (ctx, other))

    def direct(steps, half):
        return copy(0, steps, half, (later(steps), head))

    def to_upper(steps, half):
        return copy(steps, steps + 1, half, (sibling, head))

    def to_lower(steps, half):
        return copy(steps, steps - 1, half, (sibling, head))

    def spread_own(half):
        for steps in DIRECT:
            direct(steps, half).start()

        @pl.when(core == 0)
        def _():
            to_upper(0, half).start()

        @pl.when(core == 1)
        def _():
            copy(0, 7, half, (later(7), head)).start()

    def arrived(steps, half):
        copy(steps, steps, half, (ctx, other)).wait_recv()

    to_partner().start()
    spread_own(head)
    arrived(0, other)
    spread_own(other)
    for steps in DIRECT:
        for half in (head, other):
            arrived(steps, half)

            @pl.when(core == 0)
            def _():
                to_upper(steps, half).start()

            @pl.when(core == 1)
            def _():
                to_lower(steps, half).start()

    for steps in (1, 3, 5, 7):
        for half in (0, 1):
            arrived(steps, half)
    to_partner().wait_send()
    for half in (0, 1):
        for steps in DIRECT:
            direct(steps, half).wait_send()

        @pl.when(core == 0)
        def _():
            for steps in (0, 2, 4, 6):
                to_upper(steps, half).wait_send()

        @pl.when(core == 1)
        def _():
            copy(0, 7, half, (later(7), head)).wait_send()
            for steps in DIRECT:
                to_lower(steps, half).wait_send()


def attend_kernel(group, begin_ref, cos_ref, sin_ref, kv_ref, nope_ref, rope_ref, up_ref, value_ref, out_ref, bias, query, score):
    @pl.when(pl.program_id(0) == 0)
    def _():
        key = lax.broadcasted_iota(jnp.int32, (ROWS, KEYS), 1)
        row = lax.broadcasted_iota(jnp.int32, (ROWS, KEYS), 0)
        first = begin_ref[:, :1] - (lax.axis_index("ctx") - (BLOCKS - 1)) * ROWS
        live = (key >= first) & (key <= row + (KEYS - ROWS))
        bias[...] = jnp.where(live, 0.0, -1e30)

    lane = lax.broadcasted_iota(jnp.int32, (ROWS, 128), 1)
    for pair in range(group // 2):
        rope = rope_ref[:, pair * 128 : (pair + 1) * 128].astype(jnp.float32)
        swapped = jnp.where((lane & 63) < 32, pltpu.roll(rope, 96, 1), pltpu.roll(rope, 32, 1))
        turned = rope * cos_ref[...] + swapped * sin_ref[...]
        for odd in range(2):
            h = 2 * pair + odd
            own = pl.ds(h * ROWS, ROWS)
            keep = (lane >= 64) if odd else (lane < 64)
            query[own, LATENT:] = jnp.where(keep, turned, 0.0).astype(jnp.bfloat16)
            query[own, :LATENT] = jnp.dot(
                nope_ref[:, h * 128 : (h + 1) * 128], up_ref[h], preferred_element_type=jnp.float32
            ).astype(jnp.bfloat16)
    score[...] = lax.dot_general(
        query[...], kv_ref[...], (((1,), (1,)), ((), ())), preferred_element_type=jnp.float32
    )
    for h in range(group):
        s = score[pl.ds(h * ROWS, ROWS), :] + bias[...]
        top = jnp.max(s, axis=1, keepdims=True)
        weight = jnp.exp2((s - top) * (SCALE * LOG2E))
        total = jnp.sum(weight, axis=1, keepdims=True)
        mixed = jnp.dot(weight.astype(jnp.bfloat16), kv_ref[:, :LATENT], preferred_element_type=jnp.float32)
        mixed = (mixed * (1.0 / total)).astype(jnp.bfloat16)
        out_ref[:, h * 128 : (h + 1) * 128] = jnp.dot(
            mixed, value_ref[h], preferred_element_type=jnp.float32
        ).astype(jnp.bfloat16)


def shards(count, latent_raw, kv_gain, query_nope, query_rope, key_up, value_up, doc_lengths):
    vmem = pl.BlockSpec(memory_space=pltpu.VMEM)
    kv, begin, cosine, sine = pl.pallas_call(
        functools.partial(gather_kernel, count),
        out_shape=(
            jax.ShapeDtypeStruct((KEYS, WIDTH), jnp.bfloat16),
            jax.ShapeDtypeStruct((ROWS, 128), jnp.int32),
            jax.ShapeDtypeStruct((ROWS, 128), jnp.float32),
            jax.ShapeDtypeStruct((ROWS, 128), jnp.float32),
        ),
        in_specs=[vmem, vmem, pl.BlockSpec(memory_space=pltpu.SMEM)],
        out_specs=(vmem,) * 4,
        scratch_shapes=[pltpu.SemaphoreType.DMA((BLOCKS, 2)), pltpu.SemaphoreType.DMA((BLOCKS, 2))],
        compiler_params=pltpu.CompilerParams(collective_id=0, has_side_effects=True),
        name="gather_rows",
    )(latent_raw, kv_gain[None, :], doc_lengths)
    heads = key_up.shape[0]
    group = 8

    def whole(*shape):
        return pl.BlockSpec(shape, lambda i: (0,) * len(shape))

    return pl.pallas_call(
        functools.partial(attend_kernel, group),
        grid=(heads // group,),
        in_specs=[
            whole(ROWS, 128),
            whole(ROWS, 128),
            whole(ROWS, 128),
            whole(KEYS, WIDTH),
            pl.BlockSpec((ROWS, group * 128), lambda i: (0, i)),
            pl.BlockSpec((ROWS, group * 64), lambda i: (0, i)),
            pl.BlockSpec((group, 128, LATENT), lambda i: (i, 0, 0)),
            pl.BlockSpec((group, LATENT, 128), lambda i: (i, 0, 0)),
        ],
        out_specs=pl.BlockSpec((ROWS, group * 128), lambda i: (0, i)),
        out_shape=jax.ShapeDtypeStruct((ROWS, heads * 128), jnp.bfloat16),
        scratch_shapes=[
            pltpu.VMEM((ROWS, KEYS), jnp.float32),
            pltpu.VMEM((group * ROWS, WIDTH), jnp.bfloat16),
            pltpu.VMEM((group * ROWS, KEYS), jnp.float32),
        ],
        compiler_params=pltpu.CompilerParams(vmem_limit_bytes=48 << 20),
        name="attend",
    )(begin, cosine, sine, kv, query_nope, query_rope, key_up, value_up)


def solution(mesh):
    return jax.shard_map(
        functools.partial(shards, mesh.shape["ctx"]),
        mesh=mesh,
        in_specs=(
            P(("ctx", "head"), None),
            P(),
            P("ctx", "head"),
            P("ctx", "head"),
            P("head", None, None),
            P("head", None, None),
            P(),
        ),
        out_specs=P("ctx", "head"),
        check_vma=False,
    )
```

time: 184 us -> 60.2 us (0.33)
  the two profiles are of different devices: /device:TPU:128 before, /device:TPU:81 now
where the time goes in v1:
time: 60.2 us; the launch traced here: 59.8 us
  Pallas kernels  53.7 us (89%)
  local copies, waits for them, and re-layouts  6.09 us (10%)
    pallas_call x1, Pallas kernels, shards(): pl.pallas_call(functools.partial(gather_kernel, count), out_shape=(jax.Sh...  31.3 us
    pallas_call x1, Pallas kernels, shards(): pl.pallas_call(functools.partial(attend_kernel, group), grid=(heads // gr...  22.4 us
    unnamed x12, local copies, waits for them, and re-layouts  6.09 us

profile of v1, /device:TPU:81, one launch (start us, length us, event | category | flops | bytes accessed | tf_op | source)
XLA Modules:
  0.0 59.8 jit_solution(1006280325774466728)
XLA Ops:
  0.0 31.3 %gather_rows.1 = (bf16[1024,640]{1,0:T(8,128)(2,1)}, s32[128,128]{1,0:T(8,128)}, f32[128,128]{1,0:T(8,128)}, f32[128,128]{1,0:T(8,128)}) custom-call(bf16[64,576]{1,0:T(8,128)(2,1)} %raw_ref.1, f32[1,512]{1,0:T(1,128)} %bitcast.1, s32[32]{0:T(128)} %len_ref.1), custom_call_target="tpu_custom_call" | custom-call | tf_op jit(solution)/shard_map/gather_rows/pallas_call | solution.py:192
  31.3 0.0 copy-start
  31.4 1.3 %copy-done = bf16[1024,640]{1,0:T(8,128)(2,1)S(1)} copy-done((bf16[1024,640]{1,0:T(8,128)(2,1)S(1)}, bf16[1024,640]{1,0:T(8,128)(2,1)}, u32[]{:S(2)}) %copy-start) | copy-done | bytes 1310744
  32.7 0.0 copy-start.1
  32.7 1.2 %copy-done.1 = bf16[128,4096]{1,0:T(8,128)(2,1)S(1)} copy-done((bf16[128,4096]{1,0:T(8,128)(2,1)S(1)}, bf16[128,4096]{1,0:T(8,128)(2,1)}, u32[]{:S(2)}) %copy-start.1) | copy-done | bytes 1048600
  33.9 0.0 copy-start.2
  33.9 1.0 %copy-done.2 = bf16[128,2048]{1,0:T(8,128)(2,1)S(1)} copy-done((bf16[128,2048]{1,0:T(8,128)(2,1)S(1)}, bf16[128,2048]{1,0:T(8,128)(2,1)}, u32[]{:S(2)}) %copy-start.2) | copy-done | bytes 524312
  34.9 0.0 copy-start.3
  34.9 0.8 %copy-done.3 = s32[128,128]{1,0:T(8,128)S(1)} copy-done((s32[128,128]{1,0:T(8,128)S(1)}, s32[128,128]{1,0:T(8,128)}, u32[]{:S(2)}) %copy-start.3) | copy-done | bytes 65560
  35.8 0.0 copy-start.4
  35.8 0.8 %copy-done.4 = f32[128,128]{1,0:T(8,128)S(1)} copy-done((f32[128,128]{1,0:T(8,128)S(1)}, f32[128,128]{1,0:T(8,128)}, u32[]{:S(2)}) %copy-start.4) | copy-done | bytes 65560
  36.6 0.0 copy-start.5
  36.6 0.8 %copy-done.5 = f32[128,128]{1,0:T(8,128)S(1)} copy-done((f32[128,128]{1,0:T(8,128)S(1)}, f32[128,128]{1,0:T(8,128)}, u32[]{:S(2)}) %copy-start.5) | copy-done | bytes 65560
  37.4 22.4 %attend.1 = bf16[128,4096]{1,0:T(8,128)(2,1)} custom-call(s32[128,128]{1,0:T(8,128)S(1)} %copy-done.3, f32[128,128]{1,0:T(8,128)S(1)} %copy-done.4, f32[128,128]{1,0:T(8,128)S(1)} %copy-done.5, bf16[1024,640]{1,0:T(8,128)(2,1)S(1)} %copy-done, bf16[128,4096]{1,0:T(8,128)(2,1)S(1)} %copy-done.1, bf16[128,2048]{1,0:T(8,128)(2,1)S(1)} %copy-done.2, ...), custom_call_target="tpu_custom_call" | custom-call | tf_op jit(solution)/shard_map/attend/pallas_call | solution.py:212
Async XLA Ops:
  31.3 1.3 %copy-start = (bf16[1024,640]{1,0:T(8,128)(2,1)S(1)}, bf16[1024,640]{1,0:T(8,128)(2,1)}, u32[]{:S(2)}) copy-start(bf16[1024,640]{1,0:T(8,128)(2,1)} %get-tuple-element.12.kv_ref) | copy-start | bytes 3932164
  32.7 1.2 %copy-start.1 = (bf16[128,4096]{1,0:T(8,128)(2,1)S(1)}, bf16[128,4096]{1,0:T(8,128)(2,1)}, u32[]{:S(2)}) copy-start(bf16[128,4096]{1,0:T(8,128)(2,1)} %nope_ref.1) | copy-start | bytes 3145732
  33.9 1.0 %copy-start.2 = (bf16[128,2048]{1,0:T(8,128)(2,1)S(1)}, bf16[128,2048]{1,0:T(8,128)(2,1)}, u32[]{:S(2)}) copy-start(bf16[128,2048]{1,0:T(8,128)(2,1)} %rope_ref.1) | copy-start | bytes 1572868
  34.9 0.8 %copy-start.3 = (s32[128,128]{1,0:T(8,128)S(1)}, s32[128,128]{1,0:T(8,128)}, u32[]{:S(2)}) copy-start(s32[128,128]{1,0:T(8,128)} %get-tuple-element.9.begin_ref) | copy-start | bytes 196612
  35.8 0.8 %copy-start.4 = (f32[128,128]{1,0:T(8,128)S(1)}, f32[128,128]{1,0:T(8,128)}, u32[]{:S(2)}) copy-start(f32[128,128]{1,0:T(8,128)} %get-tuple-element.10.cos_ref) | copy-start | bytes 196612
  36.6 0.8 %copy-start.5 = (f32[128,128]{1,0:T(8,128)S(1)}, f32[128,128]{1,0:T(8,128)}, u32[]{:S(2)}) copy-start(f32[128,128]{1,0:T(8,128)} %get-tuple-element.11.sin_ref) | copy-start | bytes 196612

commit v2 on v1

v2 whole, which is shorter than its diff:
```python
import functools
import math

import jax
import jax.numpy as jnp
from jax import lax
from jax.experimental import pallas as pl
from jax.experimental.pallas import tpu as pltpu
from jax.sharding import PartitionSpec as P

LATENT, WIDTH = 512, 640
ROWS, HALF, BLOCKS, DOCS = 128, 64, 8, 32
KEYS = BLOCKS * ROWS
SCALE = 192.0 ** -0.5
LOG2E = math.log2(math.e)
DIRECT = (2, 4, 6)
CHUNK = 256
GROUP = 4
BAND = GROUP * ROWS
SLICE = 16
PARTS = 4
MESH = pl.DeviceIdType.MESH
WHAT = {"absorb", "score", "soft", "mix"}


def latent_attention(
    count, heads, remote, raw_ref, gain_ref, len_ref, nope_hbm, rope_hbm, up_hbm, value_hbm, out_hbm,
    kv, nope, rope, up, value, query, score, weight_a, weight_b, total_a, total_b, bias, cos_ref, sin_ref, out,
    send_sem, recv_sem, load_sem, out_sem,
):
    ctx = lax.axis_index("ctx") if remote else 0
    head = lax.axis_index("head") if remote else 0
    core = lax.rem(ctx, 2)
    other = 1 - head
    sibling = ctx + 1 - 2 * core
    per = heads // PARTS

    def later(steps):
        return lax.rem(ctx + steps, count)

    def earlier(steps):
        return lax.rem(ctx + count - steps, count)

    if remote:
        barrier = pltpu.get_barrier_semaphore()

        def greet(where):
            pl.semaphore_signal(barrier, inc=1, device_id=where, device_id_type=MESH)

        greet((ctx, other))
        greet((sibling, head))
        for steps in DIRECT:
            greet((earlier(steps), head))

        @pl.when(core == 0)
        def _():
            greet((earlier(7), head))

    def load_query():
        return pltpu.make_async_copy(nope_hbm, nope, load_sem.at[0])

    def load_rope():
        return pltpu.make_async_copy(rope_hbm, rope, load_sem.at[1])

    def load_up(part):
        own = pl.ds(part * per, per)
        return pltpu.make_async_copy(up_hbm.at[own], up.at[own], load_sem.at[2 + part])

    def load_value():
        return pltpu.make_async_copy(value_hbm, value, load_sem.at[2 + PARTS])

    load_query().start()
    load_rope().start()
    for part in range(PARTS):
        load_up(part).start()
    load_value().start()

    row = lax.broadcasted_iota(jnp.int32, (ROWS, 128), 0)
    lane = lax.broadcasted_iota(jnp.int32, (ROWS, 128), 1)
    position = ctx * ROWS + row
    begin = jnp.zeros((ROWS, 128), jnp.int32)
    start = jnp.int32(0)
    for doc in range(DOCS):
        begin = jnp.where(position >= start, start, begin)
        start = start + len_ref[doc]
    frequency = jnp.exp2((lane & 31).astype(jnp.float32) * (-math.log2(10000.0) / 32))
    angle = (position - begin).astype(jnp.float32) * frequency
    cos_ref[...] = jnp.cos(angle)
    sine = jnp.sin(angle)
    sin_ref[...] = jnp.where((lane & 63) < 32, -sine, sine)

    def half_at(steps, half):
        first = (BLOCKS - 1 - steps) * ROWS
        return pl.ds(first + pl.multiple_of(half * HALF, HALF), HALF)

    mine = half_at(0, head)
    latent = raw_ref[:, :LATENT].astype(jnp.float32)
    norm = lax.rsqrt(jnp.mean(latent * latent, axis=1, keepdims=True) + 1e-6)
    kv[mine, :LATENT] = (latent * norm * gain_ref[...]).astype(jnp.bfloat16)
    pair = raw_ref[:, LATENT:].astype(jnp.float32)
    swapped = jnp.concatenate([pair[:, 32:], pair[:, :32]], axis=1)
    table = pl.ds(pl.multiple_of(head * HALF, HALF), HALF)
    turned = pair * cos_ref[table, :64] + swapped * sin_ref[table, :64]
    kv[mine, LATENT:] = jnp.concatenate([turned, turned], axis=1).astype(jnp.bfloat16)

    def copy(source, target, half, where):
        return pltpu.make_async_remote_copy(
            src_ref=kv.at[half_at(source, half)],
            dst_ref=kv.at[half_at(target, half)],
            send_sem=send_sem.at[target, half],
            recv_sem=recv_sem.at[target, half],
            device_id=where,
            device_id_type=MESH,
        )

    def to_partner():
        return copy(0, 0, head, (ctx, other))

    def direct(steps, half):
        return copy(0, steps, half, (later(steps), head))

    def to_upper(steps, half):
        return copy(steps, steps + 1, half, (sibling, head))

    def to_lower(steps, half):
        return copy(steps, steps - 1, half, (sibling, head))

    def spread_own(half):
        for steps in DIRECT:
            direct(steps, half).start()

        @pl.when(core == 0)
        def _():
            to_upper(0, half).start()

        @pl.when(core == 1)
        def _():
            copy(0, 7, half, (later(7), head)).start()

    def arrived(steps, half):
        copy(steps, steps, half, (ctx, other)).wait_recv()

    def pass_on(steps):
        for half in (head, other):
            arrived(steps, half)

            @pl.when(core == 0)
            def _():
                to_upper(steps, half).start()

            @pl.when(core == 1)
            def _():
                to_lower(steps, half).start()

    if remote:
        pl.semaphore_wait(barrier, 5 + core)
        to_partner().start()
        spread_own(head)

    low = lane < 64
    front = (lane & 63) < 32

    def absorb(part, carry):
        load_up(part).wait()
        for p in range(per // 2):
            at = pl.multiple_of(part * (per * 64) + p * 128, 128)
            pairs = rope[:, pl.ds(at, 128)].astype(jnp.float32)
            swap = jnp.where(front, pltpu.roll(pairs, 96, 1), pltpu.roll(pairs, 32, 1))
            turn = pairs * cos_ref[...] + swap * sin_ref[...]
            for odd in range(2):
                h = part * per + 2 * p + odd
                own = pl.ds(pl.multiple_of(h * ROWS, ROWS), ROWS)
                query[own, LATENT:] = jnp.where(~low if odd else low, turn, 0.0).astype(jnp.bfloat16)
                query[own, :LATENT] = jnp.dot(
                    nope[:, pl.ds(pl.multiple_of(h * 128, 128), 128)], up[h], preferred_element_type=jnp.float32
                ).astype(jnp.bfloat16)
        return carry

    load_query().wait()
    load_rope().wait()
    if "absorb" in WHAT:
        lax.fori_loop(0, PARTS // 2, absorb, 0)
    if remote:
        arrived(0, other)
        spread_own(other)
    if "absorb" in WHAT:
        lax.fori_loop(PARTS // 2, PARTS, absorb, 0)
    else:
        for part in range(PARTS):
            load_up(part).wait()

    key = lax.broadcasted_iota(jnp.int32, (ROWS, 128), 1)
    for tile in range(BLOCKS):
        shifted = (ctx - (BLOCKS - 1) + tile) * ROWS + key
        bias[:, tile * 128 : (tile + 1) * 128] = jnp.where((shifted >= begin) & (shifted <= position), 0.0, -1e30)

    def scores(chunk):
        first = KEYS - (chunk + 1) * CHUNK

        def band(step, carry):
            own = pl.ds(pl.multiple_of(step * 1024, 1024), 1024)
            score[own, first : first + CHUNK] = lax.dot_general(
                query[own, :], kv[first : first + CHUNK, :], (((1,), (1,)), ((), ())),
                preferred_element_type=jnp.float32,
            )
            return carry

        lax.fori_loop(0, heads * ROWS // 1024, band, 0)

    for chunk in range(KEYS // CHUNK):
        if remote:
            if chunk + 1 < KEYS // CHUNK:
                pass_on(2 * chunk + 2)
            for half in (0, 1):
                arrived(2 * chunk + 1, half)
        if "score" in WHAT:
            scores(chunk)

    load_value().wait()

    def soften(step, weight, total):
        for piece in range(BAND // SLICE):
            at = piece * SLICE
            s = score[pl.ds(pl.multiple_of(step * BAND, BAND) + at, SLICE), :]
            s = s + bias[at % ROWS : at % ROWS + SLICE, :]
            top = jnp.max(s, axis=1, keepdims=True)
            w = jnp.exp2((s - top) * (SCALE * LOG2E))
            total[at : at + SLICE, :] = jnp.broadcast_to(jnp.sum(w, axis=1, keepdims=True), (SLICE, 128))
            weight[at : at + SLICE, :] = w.astype(jnp.bfloat16)

    def mix(step, weight, total):
        mixed = jnp.dot(weight[...], kv[:, :LATENT], preferred_element_type=jnp.float32)
        scale = 1.0 / total[...]
        mixed = (mixed * jnp.concatenate([scale] * (LATENT // 128), axis=1)).astype(jnp.bfloat16)
        for h in range(GROUP):
            out[:, pl.ds(pl.multiple_of(step * BAND, BAND) + h * 128, 128)] = jnp.dot(
                mixed[h * ROWS : (h + 1) * ROWS], value[step * GROUP + h], preferred_element_type=jnp.float32
            ).astype(jnp.bfloat16)
        write(step).start()

    def write(step):
        own = pl.ds(pl.multiple_of(step * BAND, BAND), BAND)
        return pltpu.make_async_copy(out.at[:, own], out_hbm.at[:, own], out_sem.at[step])

    steps = heads // GROUP
    if "soft" not in WHAT: soften = lambda *a: None
    if "mix" not in WHAT: mix = lambda s, *a: write(s).start()
    soften(0, weight_a, total_a)

    def two(j, carry):
        soften(2 * j + 1, weight_b, total_b)
        mix(2 * j, weight_a, total_a)
        soften(2 * j + 2, weight_a, total_a)
        mix(2 * j + 1, weight_b, total_b)
        return carry

    lax.fori_loop(0, steps // 2 - 1, two, 0)
    soften(steps - 1, weight_b, total_b)
    mix(steps - 2, weight_a, total_a)
    mix(steps - 1, weight_b, total_b)
    for step in range(steps):
        write(step).wait()

    if remote:
        to_partner().wait_send()
        for half in (0, 1):
            for steps in DIRECT:
                direct(steps, half).wait_send()

            @pl.when(core == 0)
            def _():
                for steps in (0, 2, 4, 6):
                    to_upper(steps, half).wait_send()

            @pl.when(core == 1)
            def _():
                copy(0, 7, half, (later(7), head)).wait_send()
                for steps in DIRECT:
                    to_lower(steps, half).wait_send()


def shards(count, remote, latent_raw, kv_gain, query_nope, query_rope, key_up, value_up, doc_lengths):
    vmem, hbm = pl.BlockSpec(memory_space=pltpu.VMEM), pl.BlockSpec(memory_space=pl.ANY)
    heads = key_up.shape[0]
    bf16, f32 = jnp.bfloat16, jnp.float32
    return pl.pallas_call(
        functools.partial(latent_attention, count, heads, remote),
        out_shape=jax.ShapeDtypeStruct((ROWS, heads * 128), bf16),
        in_specs=[vmem, vmem, pl.BlockSpec(memory_space=pltpu.SMEM), hbm, hbm, hbm, hbm],
        out_specs=hbm,
        scratch_shapes=[
            pltpu.VMEM((KEYS, WIDTH), bf16),
            pltpu.VMEM(query_nope.shape, bf16),
            pltpu.VMEM(query_rope.shape, bf16),
            pltpu.VMEM(key_up.shape, bf16),
            pltpu.VMEM(value_up.shape, bf16),
            pltpu.VMEM((heads * ROWS, WIDTH), bf16),
            pltpu.VMEM((heads * ROWS, KEYS), f32),
            pltpu.VMEM((BAND, KEYS), bf16),
            pltpu.VMEM((BAND, KEYS), bf16),
            pltpu.VMEM((BAND, 128), f32),
            pltpu.VMEM((BAND, 128), f32),
            pltpu.VMEM((ROWS, KEYS), f32),
            pltpu.VMEM((ROWS, 128), f32),
            pltpu.VMEM((ROWS, 128), f32),
            pltpu.VMEM((ROWS, heads * 128), bf16),
            pltpu.SemaphoreType.DMA((BLOCKS, 2)),
            pltpu.SemaphoreType.DMA((BLOCKS, 2)),
            pltpu.SemaphoreType.DMA((3 + PARTS,)),
            pltpu.SemaphoreType.DMA((heads // GROUP,)),
        ],
        compiler_params=pltpu.CompilerParams(
            collective_id=0 if remote else None, has_side_effects=True, vmem_limit_bytes=60 << 20
        ),
        name="latent_attention",
    )(latent_raw, kv_gain[None, :], doc_lengths, query_nope, query_rope, key_up, value_up)


def solution(mesh):
    return jax.shard_map(
        functools.partial(shards, mesh.shape["ctx"], True),
        mesh=mesh,
        in_specs=(
            P(("ctx", "head"), None),
            P(),
            P("ctx", "head"),
            P("ctx", "head"),
            P("head", None, None),
            P("head", None, None),
            P(),
        ),
        out_specs=P("ctx", "head"),
        check_vma=False,
    )
```

time: 60.2 us -> 48.9 us (0.81)
  the two profiles are of different devices: /device:TPU:81 before, /device:TPU:64 now
where the time goes in v2:
time: 48.9 us; the launch traced here: 48.8 us
  Pallas kernels  46.5 us (95%)
  local copies, waits for them, and re-layouts  2.29 us (5%)
    pallas_call x1, Pallas kernels, shards(): pl.pallas_call(functools.partial(latent_attention, count, heads, remote),...  46.5 us
    unnamed x1, local copies, waits for them, and re-layouts  2.29 us

profile of v2, /device:TPU:64, one launch (start us, length us, event | category | flops | bytes accessed | tf_op | source)
XLA Modules:
  0.0 48.8 jit_solution(8970790337000478974)
XLA Ops:
  0.0 46.5 %latent_attention.1 = bf16[128,4096]{1,0:T(8,128)(2,1)} custom-call(bf16[64,576]{1,0:T(8,128)(2,1)} %raw_ref.1, f32[1,512]{1,0:T(1,128)} %bitcast.1, s32[32]{0:T(128)} %len_ref.1, bf16[128,4096]{1,0:T(8,128)(2,1)} %nope_hbm.1, bf16[128,2048]{1,0:T(8,128)(2,1)} %rope_hbm.1, bf16[32,128,512]{2,1,0:T(8,128)(2,1)} %up_hbm.1, bf16[32,512,128]{2,1,0:T(8,128)(2,1)} %value_hbm.1), custom_call_target="tpu_custom_call" | custom-call | tf_op jit(solution)/shard_map/latent_attention/pallas_call | solution.py:286
  46.5 2.3 %copy.9 = bf16[128,4096]{1,0:T(8,128)(2,1)} copy(bf16[128,4096]{1,0:T(8,128)(2,1)} %latent_attention.1) | data formatting | bytes 2097152

commit v3 on v2

v3 whole, which is shorter than its diff:
```python
import functools
import math

import jax
import jax.numpy as jnp
from jax import lax
from jax.experimental import pallas as pl
from jax.experimental.pallas import tpu as pltpu
from jax.sharding import PartitionSpec as P

LATENT, WIDTH = 512, 640
ROWS, HALF, BLOCKS, DOCS = 128, 64, 8, 32
KEYS = BLOCKS * ROWS
SCALE = 192.0 ** -0.5
LOG2E = math.log2(math.e)
REACH = (2, 4, 6, 8)
CHUNK = 256
FAR = KEYS - CHUNK
TALL = 1024
GROUP = 4
BAND = GROUP * ROWS
SLICE = 16
PARTS = 4
MESH = pl.DeviceIdType.MESH


def latent_attention(
    count, heads, remote, raw_ref, gain_ref, len_ref, nope_hbm, rope_hbm, up_hbm, value_hbm, out_hbm,
    kv, nope, rope, up, value, query, score, peak, top_ref, sum_ref, partial, last_a, last_b, weight_a, weight_b,
    narrow_a, narrow_b, old_a, old_b, new_a, new_b, bias, cos_ref, sin_ref, out,
    send_sem, recv_sem, load_sem, out_sem,
):
    ctx = lax.axis_index("ctx") if remote else 0
    head = lax.axis_index("head") if remote else 0
    core = lax.rem(ctx, 2)
    other = 1 - head
    sibling = ctx + 1 - 2 * core
    per = heads // PARTS

    def has_behind(steps):
        return ctx >= steps

    def has_ahead(steps):
        return ctx + steps < count

    if remote:
        barrier = pltpu.get_barrier_semaphore()

        def greet(where):
            pl.semaphore_signal(barrier, inc=1, device_id=where, device_id_type=MESH)

        @pl.when(ctx < BLOCKS)
        def _():
            kv[...] = jnp.zeros_like(kv)

        greet((ctx, other))
        greet((sibling, head))
        for steps in REACH:

            @pl.when(has_behind(steps))
            def _():
                for plane in (0, 1):
                    greet((ctx - steps, plane))

    def load_query():
        return pltpu.make_async_copy(nope_hbm, nope, load_sem.at[0])

    def load_rope():
        return pltpu.make_async_copy(rope_hbm, rope, load_sem.at[1])

    def load_up(part):
        own = pl.ds(part * per, per)
        return pltpu.make_async_copy(up_hbm.at[own], up.at[own], load_sem.at[2 + part])

    def load_value():
        return pltpu.make_async_copy(value_hbm, value, load_sem.at[2 + PARTS])

    load_query().start()
    load_rope().start()
    for part in range(PARTS):
        load_up(part).start()
    load_value().start()

    row = lax.broadcasted_iota(jnp.int32, (ROWS, 128), 0)
    lane = lax.broadcasted_iota(jnp.int32, (ROWS, 128), 1)
    position = ctx * ROWS + row
    begin = jnp.zeros((ROWS, 128), jnp.int32)
    start = jnp.int32(0)
    for doc in range(DOCS):
        begin = jnp.where(position >= start, start, begin)
        start = start + len_ref[doc]
    frequency = jnp.exp2((lane & 31).astype(jnp.float32) * (-math.log2(10000.0) / 32))
    angle = (position - begin).astype(jnp.float32) * frequency
    cos_ref[...] = jnp.cos(angle)
    sine = jnp.sin(angle)
    sin_ref[...] = jnp.where((lane & 63) < 32, -sine, sine)

    def half_at(steps, half):
        return pl.ds(pl.multiple_of((BLOCKS - steps) * ROWS + half * HALF, HALF), HALF)

    mine = half_at(0, head)
    latent = raw_ref[:, :LATENT].astype(jnp.float32)
    norm = lax.rsqrt(jnp.mean(latent * latent, axis=1, keepdims=True) + 1e-6)
    kv[mine, :LATENT] = (latent * norm * gain_ref[...]).astype(jnp.bfloat16)
    pair = raw_ref[:, LATENT:].astype(jnp.float32)
    swapped = jnp.concatenate([pair[:, 32:], pair[:, :32]], axis=1)
    table = pl.ds(pl.multiple_of(head * HALF, HALF), HALF)
    turned = pair * cos_ref[table, :64] + swapped * sin_ref[table, :64]
    kv[mine, LATENT:] = jnp.concatenate([turned, turned], axis=1).astype(jnp.bfloat16)

    def copy(source, target, half, where, send):
        return pltpu.make_async_remote_copy(
            src_ref=kv.at[half_at(source, half)],
            dst_ref=kv.at[half_at(target, half)],
            send_sem=send_sem.at[send],
            recv_sem=recv_sem.at[target, half],
            device_id=where,
            device_id_type=MESH,
        )

    def to_partner():
        return copy(0, 0, head, (ctx, other), 0)

    def direct(steps, plane):
        return copy(0, steps, head, (ctx + steps, plane), steps - 1 + plane)

    def across(steps, half):
        source = jnp.where((core == 1) & (steps == 0), BLOCKS, steps)
        target = jnp.where(core == 0, steps + 1, jnp.where(steps == 0, BLOCKS - 1, steps - 1))
        return copy(source, target, half, (sibling, head), 9 + steps + half)

    def arrived(steps, half):
        copy(steps, steps, half, (ctx, other), 0).wait_recv()

    def spread(steps):
        @pl.when(has_ahead(steps))
        def _():
            for plane in (0, 1):
                direct(steps, plane).start()

    def landed(steps):
        @pl.when(has_behind(steps))
        def _():
            for half in (0, 1):
                arrived(steps, half)

    def pass_on(steps):
        landed(steps)
        for half in (0, 1):
            across(steps, half).start()

    def pass_ends(lower):
        @pl.when(core == (1 if lower else 0))
        def _():
            for half in (0, 1):
                across(0, half).start()

    if remote:
        reached = sum(has_ahead(steps).astype(jnp.int32) for steps in REACH)
        pl.semaphore_wait(barrier, 2 + 2 * reached)
        to_partner().start()
        spread(2)
        spread(4)
        spread(6)
        spread(8)

    low = lane < 64
    front = (lane & 63) < 32

    def absorb(part, carry):
        load_up(part).wait()
        for p in range(per // 2):
            at = pl.multiple_of(part * (per * 64) + p * 128, 128)
            pairs = rope[:, pl.ds(at, 128)].astype(jnp.float32)
            swap = jnp.where(front, pltpu.roll(pairs, 96, 1), pltpu.roll(pairs, 32, 1))
            turn = pairs * cos_ref[...] + swap * sin_ref[...]
            for odd in range(2):
                h = part * per + 2 * p + odd
                own = pl.ds(pl.multiple_of(h * ROWS, ROWS), ROWS)
                query[own, LATENT:] = jnp.where(~low if odd else low, turn, 0.0).astype(jnp.bfloat16)
                query[own, :LATENT] = jnp.dot(
                    nope[:, pl.ds(pl.multiple_of(h * 128, 128), 128)], up[h], preferred_element_type=jnp.float32
                ).astype(jnp.bfloat16)
        return carry

    key = lax.broadcasted_iota(jnp.int32, (ROWS, 128), 1)
    for tile in range(BLOCKS):
        shifted = (ctx - (BLOCKS - 1) + tile) * ROWS + key
        bias[:, tile * 128 : (tile + 1) * 128] = jnp.where((shifted >= begin) & (shifted <= position), 0.0, -1e30)

    load_query().wait()
    load_rope().wait()
    for part in range(PARTS):
        lax.fori_loop(part, part + 1, absorb, 0)
    if remote:
        arrived(0, other)

    def scores(chunk):
        first = FAR - (chunk + 1) * CHUNK

        def band(step, carry):
            own = pl.ds(pl.multiple_of(step * TALL, TALL), TALL)
            s = lax.dot_general(
                query[own, :], kv[ROWS + CHUNK + first : ROWS + 2 * CHUNK + first, :], (((1,), (1,)), ((), ())),
                preferred_element_type=jnp.float32,
            )
            s = s.reshape(TALL // ROWS, ROWS, CHUNK) * (SCALE * LOG2E)
            s = (s + bias[:, CHUNK + first : 2 * CHUNK + first]).reshape(TALL, CHUNK)
            score[own, first : first + CHUNK] = s
            high = jnp.maximum(s[:, :128], s[:, 128:])
            peak[own, :] = jnp.maximum(peak[own, :], high) if chunk else high
            return carry

        lax.fori_loop(0, heads * ROWS // TALL, band, 0)

    def soften(step, weight):
        for piece in range(BAND // SLICE):
            at = piece * SLICE
            own = pl.ds(pl.multiple_of(step * BAND, BAND) + at, SLICE)
            top = jnp.broadcast_to(jnp.max(peak[own, :], axis=1, keepdims=True), (SLICE, 128))
            total = None
            for tile in range(FAR // 128):
                w = jnp.exp2(score[own, tile * 128 : (tile + 1) * 128] - top)
                total = w if total is None else total + w
                weight[at : at + SLICE, tile * 128 : (tile + 1) * 128] = w.astype(jnp.bfloat16)
            top_ref[own, :] = top
            sum_ref[own, :] = total

    def mix(step, weight):
        partial[pl.ds(pl.multiple_of(step * BAND, BAND), BAND), :] = jnp.dot(
            weight[...], kv[ROWS + CHUNK :, :LATENT], preferred_element_type=jnp.float32
        )

    def score_far(step, last):
        own = pl.ds(pl.multiple_of(step * BAND, BAND), BAND)
        s = lax.dot_general(
            query[own, :], kv[ROWS : ROWS + CHUNK, :], (((1,), (1,)), ((), ())), preferred_element_type=jnp.float32
        )
        s = s.reshape(GROUP, ROWS, CHUNK) * (SCALE * LOG2E) + bias[:, :CHUNK]
        last[...] = s.reshape(BAND, CHUNK)

    def soften_far(step, last, narrow, old, new):
        for piece in range(BAND // SLICE):
            at = piece * SLICE
            own = pl.ds(pl.multiple_of(step * BAND, BAND) + at, SLICE)
            s0, s1 = last[at : at + SLICE, :128], last[at : at + SLICE, 128:]
            before = top_ref[own, :]
            high = jnp.maximum(jnp.maximum(s0, s1), before)
            top = jnp.broadcast_to(jnp.max(high, axis=1, keepdims=True), (SLICE, 128))
            w0, w1 = jnp.exp2(s0 - top), jnp.exp2(s1 - top)
            fade = jnp.exp2(before - top)
            total = jnp.sum(sum_ref[own, :] * fade + w0 + w1, axis=1, keepdims=True)
            scale = jnp.broadcast_to(1.0 / total, (SLICE, 128))
            narrow[at : at + SLICE, :128] = w0.astype(jnp.bfloat16)
            narrow[at : at + SLICE, 128:] = w1.astype(jnp.bfloat16)
            new[at : at + SLICE, :] = scale
            old[at : at + SLICE, :] = scale * fade

    def finish(step, narrow, old, new):
        own = pl.ds(pl.multiple_of(step * BAND, BAND), BAND)
        mixed = jnp.dot(narrow[...], kv[ROWS : ROWS + CHUNK, :LATENT], preferred_element_type=jnp.float32)
        a, b = old[...], new[...]
        mixed = jnp.concatenate(
            [
                (partial[own, t : t + 128] * a + mixed[:, t : t + 128] * b).astype(jnp.bfloat16)
                for t in range(0, LATENT, 128)
            ],
            axis=1,
        )
        for h in range(GROUP):
            out[:, pl.ds(pl.multiple_of(step * BAND, BAND) + h * 128, 128)] = jnp.dot(
                mixed[h * ROWS : (h + 1) * ROWS], value[step * GROUP + h], preferred_element_type=jnp.float32
            ).astype(jnp.bfloat16)
        write(step).start()

    def write(step):
        own = pl.ds(pl.multiple_of(step * BAND, BAND), BAND)
        return pltpu.make_async_copy(out.at[:, own], out_hbm.at[:, own], out_sem.at[step])

    steps = heads // GROUP
    for chunk in range(KEYS // CHUNK):
        if remote:
            if chunk == 0:
                pass_ends(False)
            for steps_on in ((2, 4), (6,), (), ())[chunk]:
                pass_on(steps_on)
            if chunk == 2:
                landed(BLOCKS)
                pass_ends(True)
            for half in (0, 1):
                arrived(2 * chunk + 1, half)
        if chunk + 1 < KEYS // CHUNK:
            scores(chunk)
        if chunk + 2 == KEYS // CHUNK:
            soften(0, weight_a)

            def near(j, carry):
                soften(2 * j + 1, weight_b)
                mix(2 * j, weight_a)
                soften(2 * j + 2, weight_a)
                mix(2 * j + 1, weight_b)
                return carry

            lax.fori_loop(0, steps // 2 - 1, near, 0)
            soften(steps - 1, weight_b)
            mix(steps - 2, weight_a)
            mix(steps - 1, weight_b)

    load_value().wait()
    even, odd = (narrow_a, old_a, new_a), (narrow_b, old_b, new_b)
    score_far(0, last_a)
    score_far(1, last_b)
    soften_far(0, last_a, *even)

    def far(j, carry):
        score_far(2 * j + 2, last_a)
        soften_far(2 * j + 1, last_b, *odd)
        finish(2 * j, *even)
        score_far(2 * j + 3, last_b)
        soften_far(2 * j + 2, last_a, *even)
        finish(2 * j + 1, *odd)
        return carry

    lax.fori_loop(0, steps // 2 - 1, far, 0)
    soften_far(steps - 1, last_b, *odd)
    finish(steps - 2, *even)
    finish(steps - 1, *odd)
    for step in range(steps):
        write(step).wait()

    if remote:
        to_partner().wait_send()
        for half in (0, 1):
            for steps in REACH:

                @pl.when(has_ahead(steps))
                def _():
                    direct(steps, half).wait_send()

            for steps in (0, 2, 4, 6):
                across(steps, half).wait_send()


def shards(count, remote, latent_raw, kv_gain, query_nope, query_rope, key_up, value_up, doc_lengths):
    vmem, hbm = pl.BlockSpec(memory_space=pltpu.VMEM), pl.BlockSpec(memory_space=pl.ANY)
    heads = key_up.shape[0]
    bf16, f32 = jnp.bfloat16, jnp.float32
    return pl.pallas_call(
        functools.partial(latent_attention, count, heads, remote),
        out_shape=jax.ShapeDtypeStruct((ROWS, heads * 128), bf16),
        in_specs=[vmem, vmem, pl.BlockSpec(memory_space=pltpu.SMEM), hbm, hbm, hbm, hbm],
        out_specs=hbm,
        scratch_shapes=[
            pltpu.VMEM((ROWS + KEYS, WIDTH), bf16),
            pltpu.VMEM(query_nope.shape, bf16),
            pltpu.VMEM(query_rope.shape, bf16),
            pltpu.VMEM(key_up.shape, bf16),
            pltpu.VMEM(value_up.shape, bf16),
            pltpu.VMEM((heads * ROWS, WIDTH), bf16),
            pltpu.VMEM((heads * ROWS, FAR), f32),
            *[pltpu.VMEM((heads * ROWS, 128), f32)] * 3,
            pltpu.VMEM((heads * ROWS, LATENT), f32),
            *[pltpu.VMEM((BAND, CHUNK), f32)] * 2,
            *[pltpu.VMEM((BAND, FAR), bf16)] * 2,
            *[pltpu.VMEM((BAND, CHUNK), bf16)] * 2,
            *[pltpu.VMEM((BAND, 128), f32)] * 4,
            pltpu.VMEM((ROWS, KEYS), f32),
            pltpu.VMEM((ROWS, 128), f32),
            pltpu.VMEM((ROWS, 128), f32),
            pltpu.VMEM((ROWS, heads * 128), bf16),
            pltpu.SemaphoreType.DMA((23,)),
            pltpu.SemaphoreType.DMA((BLOCKS + 1, 2)),
            pltpu.SemaphoreType.DMA((3 + PARTS,)),
            pltpu.SemaphoreType.DMA((heads // GROUP,)),
        ],
        compiler_params=pltpu.CompilerParams(
            collective_id=0 if remote else None, has_side_effects=True, vmem_limit_bytes=60 << 20
        ),
        name="latent_attention",
    )(latent_raw, kv_gain[None, :], doc_lengths, query_nope, query_rope, key_up, value_up)


def solution(mesh):
    return jax.shard_map(
        functools.partial(shards, mesh.shape["ctx"], True),
        mesh=mesh,
        in_specs=(
            P(("ctx", "head"), None),
            P(),
            P("ctx", "head"),
            P("ctx", "head"),
            P("head", None, None),
            P("head", None, None),
            P(),
        ),
        out_specs=P("ctx", "head"),
        check_vma=False,
    )
```

time: 48.9 us -> 39.3 us (0.80)
  the two profiles are of different devices: /device:TPU:64 before, /device:TPU:140 now
where the time goes in v3:
time: 39.3 us; the launch traced here: 39.2 us
  Pallas kernels  36.9 us (94%)
  local copies, waits for them, and re-layouts  2.29 us (6%)
    pallas_call x1, Pallas kernels, shards(): pl.pallas_call(functools.partial(latent_attention, count, heads, remote),...  36.9 us
    unnamed x1, local copies, waits for them, and re-layouts  2.29 us

profile of v3, /device:TPU:140, one launch (start us, length us, event | category | flops | bytes accessed | tf_op | source)
XLA Modules:
  0.0 39.2 jit_solution(14418387916709351453)
XLA Ops:
  0.0 36.9 %latent_attention.1 = bf16[128,4096]{1,0:T(8,128)(2,1)} custom-call(bf16[64,576]{1,0:T(8,128)(2,1)} %raw_ref.1, f32[1,512]{1,0:T(1,128)} %bitcast.1, s32[32]{0:T(128)} %len_ref.1, bf16[128,4096]{1,0:T(8,128)(2,1)} %nope_hbm.1, bf16[128,2048]{1,0:T(8,128)(2,1)} %rope_hbm.1, bf16[32,128,512]{2,1,0:T(8,128)(2,1)} %up_hbm.1, bf16[32,512,128]{2,1,0:T(8,128)(2,1)} %value_hbm.1), custom_call_target="tpu_custom_call" | custom-call | tf_op jit(solution)/shard_map/latent_attention/pallas_call | solution.py:348
  36.9 2.3 %copy.9 = bf16[128,4096]{1,0:T(8,128)(2,1)} copy(bf16[128,4096]{1,0:T(8,128)(2,1)} %latent_attention.1) | data formatting | bytes 2097152

commit v4 on v3

--- a/solution.py
+++ b/solution.py
@@ -15,12 +15,13 @@
 LOG2E = math.log2(math.e)
 REACH = (2, 4, 6, 8)
 CHUNK = 256
-FAR = KEYS - CHUNK
-TALL = 1024
+NEAR = 512
+FAR = KEYS - NEAR
+TALL = 2048
 GROUP = 4
 BAND = GROUP * ROWS
 SLICE = 16
-PARTS = 4
+PARTS = 8
 MESH = pl.DeviceIdType.MESH
 
 
@@ -37,11 +38,14 @@
     sibling = ctx + 1 - 2 * core
     per = heads // PARTS
 
+    def wanted(steps):
+        return core == 1 if steps == BLOCKS else core >= 0
+
     def has_behind(steps):
-        return ctx >= steps
+        return jnp.logical_and(ctx >= steps, wanted(steps))
 
     def has_ahead(steps):
-        return ctx + steps < count
+        return jnp.logical_and(ctx + steps < count, wanted(steps))
 
     if remote:
         barrier = pltpu.get_barrier_semaphore()
@@ -190,22 +194,21 @@
 
     load_query().wait()
     load_rope().wait()
-    for part in range(PARTS):
-        lax.fori_loop(part, part + 1, absorb, 0)
+    lax.fori_loop(0, PARTS, absorb, 0)
     if remote:
         arrived(0, other)
 
     def scores(chunk):
-        first = FAR - (chunk + 1) * CHUNK
+        first = NEAR - (chunk + 1) * CHUNK
 
         def band(step, carry):
             own = pl.ds(pl.multiple_of(step * TALL, TALL), TALL)
             s = lax.dot_general(
-                query[own, :], kv[ROWS + CHUNK + first : ROWS + 2 * CHUNK + first, :], (((1,), (1,)), ((), ())),
+                query[own, :], kv[ROWS + FAR + first : ROWS + FAR + first + CHUNK, :], (((1,), (1,)), ((), ())),
                 preferred_element_type=jnp.float32,
             )
             s = s.reshape(TALL // ROWS, ROWS, CHUNK) * (SCALE * LOG2E)
-            s = (s + bias[:, CHUNK + first : 2 * CHUNK + first]).reshape(TALL, CHUNK)
+            s = (s + bias[:, FAR + first : FAR + first + CHUNK]).reshape(TALL, CHUNK)
             score[own, first : first + CHUNK] = s
             high = jnp.maximum(s[:, :128], s[:, 128:])
             peak[own, :] = jnp.maximum(peak[own, :], high) if chunk else high
@@ -219,7 +222,7 @@
             own = pl.ds(pl.multiple_of(step * BAND, BAND) + at, SLICE)
             top = jnp.broadcast_to(jnp.max(peak[own, :], axis=1, keepdims=True), (SLICE, 128))
             total = None
-            for tile in range(FAR // 128):
+            for tile in range(NEAR // 128):
                 w = jnp.exp2(score[own, tile * 128 : (tile + 1) * 128] - top)
                 total = w if total is None else total + w
                 weight[at : at + SLICE, tile * 128 : (tile + 1) * 128] = w.astype(jnp.bfloat16)
@@ -228,37 +231,40 @@
 
     def mix(step, weight):
         partial[pl.ds(pl.multiple_of(step * BAND, BAND), BAND), :] = jnp.dot(
-            weight[...], kv[ROWS + CHUNK :, :LATENT], preferred_element_type=jnp.float32
+            weight[...], kv[ROWS + FAR :, :LATENT], preferred_element_type=jnp.float32
         )
 
     def score_far(step, last):
         own = pl.ds(pl.multiple_of(step * BAND, BAND), BAND)
         s = lax.dot_general(
-            query[own, :], kv[ROWS : ROWS + CHUNK, :], (((1,), (1,)), ((), ())), preferred_element_type=jnp.float32
+            query[own, :], kv[ROWS : ROWS + FAR, :], (((1,), (1,)), ((), ())), preferred_element_type=jnp.float32
         )
-        s = s.reshape(GROUP, ROWS, CHUNK) * (SCALE * LOG2E) + bias[:, :CHUNK]
-        last[...] = s.reshape(BAND, CHUNK)
+        s = s.reshape(GROUP, ROWS, FAR) * (SCALE * LOG2E) + bias[:, :FAR]
+        last[...] = s.reshape(BAND, FAR)
 
     def soften_far(step, last, narrow, old, new):
         for piece in range(BAND // SLICE):
             at = piece * SLICE
             own = pl.ds(pl.multiple_of(step * BAND, BAND) + at, SLICE)
-            s0, s1 = last[at : at + SLICE, :128], last[at : at + SLICE, 128:]
             before = top_ref[own, :]
-            high = jnp.maximum(jnp.maximum(s0, s1), before)
+            high = before
+            for tile in range(0, FAR, 128):
+                high = jnp.maximum(high, last[at : at + SLICE, tile : tile + 128])
             top = jnp.broadcast_to(jnp.max(high, axis=1, keepdims=True), (SLICE, 128))
-            w0, w1 = jnp.exp2(s0 - top), jnp.exp2(s1 - top)
             fade = jnp.exp2(before - top)
-            total = jnp.sum(sum_ref[own, :] * fade + w0 + w1, axis=1, keepdims=True)
+            total = sum_ref[own, :] * fade
+            for tile in range(0, FAR, 128):
+                w = jnp.exp2(last[at : at + SLICE, tile : tile + 128] - top)
+                total = total + w
+                narrow[at : at + SLICE, tile : tile + 128] = w.astype(jnp.bfloat16)
+            total = jnp.sum(total, axis=1, keepdims=True)
             scale = jnp.broadcast_to(1.0 / total, (SLICE, 128))
-            narrow[at : at + SLICE, :128] = w0.astype(jnp.bfloat16)
-            narrow[at : at + SLICE, 128:] = w1.astype(jnp.bfloat16)
             new[at : at + SLICE, :] = scale
             old[at : at + SLICE, :] = scale * fade
 
     def finish(step, narrow, old, new):
         own = pl.ds(pl.multiple_of(step * BAND, BAND), BAND)
-        mixed = jnp.dot(narrow[...], kv[ROWS : ROWS + CHUNK, :LATENT], preferred_element_type=jnp.float32)
+        mixed = jnp.dot(narrow[...], kv[ROWS : ROWS + FAR, :LATENT], preferred_element_type=jnp.float32)
         a, b = old[...], new[...]
         mixed = jnp.concatenate(
             [
@@ -284,14 +290,14 @@
                 pass_ends(False)
             for steps_on in ((2, 4), (6,), (), ())[chunk]:
                 pass_on(steps_on)
-            if chunk == 2:
-                landed(BLOCKS)
-                pass_ends(True)
             for half in (0, 1):
                 arrived(2 * chunk + 1, half)
-        if chunk + 1 < KEYS // CHUNK:
+        if chunk < NEAR // CHUNK:
             scores(chunk)
-        if chunk + 2 == KEYS // CHUNK:
+        if remote and chunk == 1:
+            landed(BLOCKS)
+            pass_ends(True)
+        if chunk + 1 == NEAR // CHUNK:
             soften(0, weight_a)
 
             def near(j, carry):
@@ -357,12 +363,12 @@
             pltpu.VMEM(key_up.shape, bf16),
             pltpu.VMEM(value_up.shape, bf16),
             pltpu.VMEM((heads * ROWS, WIDTH), bf16),
-            pltpu.VMEM((heads * ROWS, FAR), f32),
+            pltpu.VMEM((heads * ROWS, NEAR), f32),
             *[pltpu.VMEM((heads * ROWS, 128), f32)] * 3,
             pltpu.VMEM((heads * ROWS, LATENT), f32),
-            *[pltpu.VMEM((BAND, CHUNK), f32)] * 2,
+            *[pltpu.VMEM((BAND, FAR), f32)] * 2,
+            *[pltpu.VMEM((BAND, NEAR), bf16)] * 2,
             *[pltpu.VMEM((BAND, FAR), bf16)] * 2,
-            *[pltpu.VMEM((BAND, CHUNK), bf16)] * 2,
             *[pltpu.VMEM((BAND, 128), f32)] * 4,
             pltpu.VMEM((ROWS, KEYS), f32),
             pltpu.VMEM((ROWS, 128), f32),

time: 39.3 us -> 38.2 us (0.972)
  Pallas kernels: 36.9 us -> 35.7 us
    pallas_call x1, Pallas kernels: 36.9 us -> 35.7 us  [shards(): pl.pallas_call(functools.partial(latent_attention, count, heads, remote),...]
where the time goes in v4:
time: 38.2 us; the launch traced here: 38 us
  Pallas kernels  35.7 us (93%)
  local copies, waits for them, and re-layouts  2.29 us (6%)
    pallas_call x1, Pallas kernels, shards(): pl.pallas_call(functools.partial(latent_attention, count, heads, remote),...  35.7 us
    unnamed x1, local copies, waits for them, and re-layouts  2.29 us

profile of v4, /device:TPU:140, one launch (start us, length us, event | category | flops | bytes accessed | tf_op | source)
XLA Modules:
  0.0 38.0 jit_solution(11071490431309471673)
XLA Ops:
  0.0 35.7 %latent_attention.1 = bf16[128,4096]{1,0:T(8,128)(2,1)} custom-call(bf16[64,576]{1,0:T(8,128)(2,1)} %raw_ref.1, f32[1,512]{1,0:T(1,128)} %bitcast.1, s32[32]{0:T(128)} %len_ref.1, bf16[128,4096]{1,0:T(8,128)(2,1)} %nope_hbm.1, bf16[128,2048]{1,0:T(8,128)(2,1)} %rope_hbm.1, bf16[32,128,512]{2,1,0:T(8,128)(2,1)} %up_hbm.1, bf16[32,512,128]{2,1,0:T(8,128)(2,1)} %value_hbm.1), custom_call_target="tpu_custom_call" | custom-call | tf_op jit(solution)/shard_map/latent_attention/pallas_call | solution.py:354
  35.7 2.3 %copy.9 = bf16[128,4096]{1,0:T(8,128)(2,1)} copy(bf16[128,4096]{1,0:T(8,128)(2,1)} %latent_attention.1) | data formatting | bytes 2097152

commit v5 on v4

--- a/solution.py
+++ b/solution.py
@@ -139,7 +139,7 @@
     def spread(steps):
         @pl.when(has_ahead(steps))
         def _():
-            for plane in (0, 1):
+            for plane in (head, other):
                 direct(steps, plane).start()
 
     def landed(steps):
@@ -288,7 +288,7 @@
         if remote:
             if chunk == 0:
                 pass_ends(False)
-            for steps_on in ((2, 4), (6,), (), ())[chunk]:
+            for steps_on in ((2,), (4, 6), (), ())[chunk]:
                 pass_on(steps_on)
             for half in (0, 1):
                 arrived(2 * chunk + 1, half)

time: 38.2 us -> 37.6 us (0.984)
  the two profiles are of different devices: /device:TPU:140 before, /device:TPU:144 now
where the time goes in v5:
time: 37.6 us; the launch traced here: 37.4 us
  Pallas kernels  35.1 us (93%)
  local copies, waits for them, and re-layouts  2.29 us (6%)
    pallas_call x1, Pallas kernels, shards(): pl.pallas_call(functools.partial(latent_attention, count, heads, remote),...  35.1 us
    unnamed x1, local copies, waits for them, and re-layouts  2.29 us

profile of v5, /device:TPU:144, one launch (start us, length us, event | category | flops | bytes accessed | tf_op | source)
XLA Modules:
  0.0 37.4 jit_solution(11407335517902562546)
XLA Ops:
  0.0 35.1 %latent_attention.1 = bf16[128,4096]{1,0:T(8,128)(2,1)} custom-call(bf16[64,576]{1,0:T(8,128)(2,1)} %raw_ref.1, f32[1,512]{1,0:T(1,128)} %bitcast.1, s32[32]{0:T(128)} %len_ref.1, bf16[128,4096]{1,0:T(8,128)(2,1)} %nope_hbm.1, bf16[128,2048]{1,0:T(8,128)(2,1)} %rope_hbm.1, bf16[32,128,512]{2,1,0:T(8,128)(2,1)} %up_hbm.1, bf16[32,512,128]{2,1,0:T(8,128)(2,1)} %value_hbm.1), custom_call_target="tpu_custom_call" | custom-call | tf_op jit(solution)/shard_map/latent_attention/pallas_call | solution.py:354
  35.1 2.3 %copy.9 = bf16[128,4096]{1,0:T(8,128)(2,1)} copy(bf16[128,4096]{1,0:T(8,128)(2,1)} %latent_attention.1) | data formatting | bytes 2097152

commit v6 on v5

--- a/solution.py
+++ b/solution.py
@@ -162,8 +162,8 @@
     if remote:
         reached = sum(has_ahead(steps).astype(jnp.int32) for steps in REACH)
         pl.semaphore_wait(barrier, 2 + 2 * reached)
+        spread(2)
         to_partner().start()
-        spread(2)
         spread(4)
         spread(6)
         spread(8)

time: 37.6 us -> 37.6 us (level)
  no operation moved by 1% of the time
where the time goes in v6:
time: 37.6 us; the launch traced here: 37.4 us
  Pallas kernels  35.1 us (93%)
  local copies, waits for them, and re-layouts  2.29 us (6%)
    pallas_call x1, Pallas kernels, shards(): pl.pallas_call(functools.partial(latent_attention, count, heads, remote),...  35.1 us
    unnamed x1, local copies, waits for them, and re-layouts  2.29 us

profile of v6, /device:TPU:144, one launch (start us, length us, event | category | flops | bytes accessed | tf_op | source)
XLA Modules:
  0.0 37.4 jit_solution(16934999998117973333)
XLA Ops:
  0.0 35.1 %latent_attention.1 = bf16[128,4096]{1,0:T(8,128)(2,1)} custom-call(bf16[64,576]{1,0:T(8,128)(2,1)} %raw_ref.1, f32[1,512]{1,0:T(1,128)} %bitcast.1, s32[32]{0:T(128)} %len_ref.1, bf16[128,4096]{1,0:T(8,128)(2,1)} %nope_hbm.1, bf16[128,2048]{1,0:T(8,128)(2,1)} %rope_hbm.1, bf16[32,128,512]{2,1,0:T(8,128)(2,1)} %up_hbm.1, bf16[32,512,128]{2,1,0:T(8,128)(2,1)} %value_hbm.1), custom_call_target="tpu_custom_call" | custom-call | tf_op jit(solution)/shard_map/latent_attention/pallas_call | solution.py:354
  35.1 2.3 %copy.9 = bf16[128,4096]{1,0:T(8,128)(2,1)} copy(bf16[128,4096]{1,0:T(8,128)(2,1)} %latent_attention.1) | data formatting | bytes 2097152
